TPU v7x, 512 devices: a whole 4x8x8 slice. The times are simulated.
512 devices in a mesh: rec: 128 (over y, z, core), grp: 4 (over x).
Axes of the slice: x: 4, y: 8, z: 8, core: 2. Of those that a mesh axis runs over, the one named last changes fastest.
Arguments:
- conv_in: bfloat16 [4, 131072, 512], P('grp', 'rec'), may hold values from -6 to 6
- conv5_weight: bfloat16 [1536, 512], P(None, 'grp'), may hold values from -0.15625 to 0.15625
- conv6_weight: bfloat16 [1024, 512], P(None, 'grp'), may hold values from -0.1875 to 0.1875
- conv7_weight: bfloat16 [1024, 512], P(None, 'grp'), may hold values from -0.1875 to 0.1875
- norm_gain: float32 [512], replicated, may hold values from 0.1 to 1.9
- norm_bias: float32 [512], replicated, may hold values from -3 to 3
- proj_weight: bfloat16 [512, 768], P(None, 'grp'), may hold values from -0.25 to 0.25
- proj_bias: float32 [768], replicated, may hold values from -3 to 3
- rec_length: int32 [4], P('grp'), may hold values from 8192 to 16384, as said below
- assign: int32 [3, 4, 16384], P(None, 'grp', 'rec'), may hold values from 0 to 999, as said below
- centroid_init: float32 [1024, 768], P('rec'), may hold values from -6 to 6
- prior_count: float32 [1024], P('rec'), may hold values from 50 to 500
Outputs:
- distortion: float32 [3, 4, 16384], P(None, 'grp', 'rec')
- centroids: float32 [1024, 768], P('rec')
Inputs may be any that keep to these rules, and one draw needn't show every extreme that they name: `rec_length`: some recording has all 16384 frames. `assign`: clusters form blocks of 8 consecutive ids (block b holds ids b * 8 to b * 8 + 7). In each iteration the 128 frames of one device name clusters of one block at most 2 times, and in each iteration some block is named exactly 2 times by the frames of every device of one recording.
All inputs are finite; a program needn't handle non-finite values.
Results may differ from a plain program's by a relative error of at most 0.0013.
Values may be sent and summed in bfloat16 or wider, within the bound.
A program may use at most 64 MiB of HBM per device.

v0:
```python
import jax
import jax.numpy as jnp
from jax import lax
from jax.sharding import PartitionSpec as P

K = 1000
ITERS = 3


def shifted(value, axis, steps):
    count = lax.axis_size(axis)
    initial, last = (max(0, -steps), min(count, count - steps))
    return lax.ppermute(value, axis, [(source, source + steps) for source in range(initial, last)])


def linear(inputs, weight):
    return jnp.dot(
        inputs,
        lax.all_gather(weight, "grp", axis=1, tiled=True),
        preferred_element_type=jnp.float32,
    )


def conv_layer(inputs, weight):
    return jax.nn.gelu(linear(inputs, weight), approximate=False).astype(jnp.bfloat16)


def shards(
    conv_in,
    conv5_weight,
    conv6_weight,
    conv7_weight,
    norm_gain,
    norm_bias,
    proj_weight,
    proj_bias,
    rec_length,
    assign,
    centroid_init,
    prior_count,
):
    signal = conv_in[0]
    sample_rows = signal.shape[0]
    channels = signal.shape[1]
    next_row = shifted(signal[:1], "rec", -1)
    paired = signal.reshape(sample_rows // 2, 2 * channels)
    trailing = jnp.concatenate([signal[2::2], next_row], 0)
    stacked = jnp.concatenate([paired, trailing], 1)
    hidden = conv_layer(stacked, conv5_weight)
    hidden = conv_layer(hidden.reshape(-1, 2 * channels), conv6_weight)
    hidden = conv_layer(hidden.reshape(-1, 2 * channels), conv7_weight)
    hidden_wide = hidden.astype(jnp.float32)
    average = jnp.mean(hidden_wide, axis=-1, keepdims=True)
    variance = jnp.mean((hidden_wide - average) ** 2, axis=-1, keepdims=True)
    normed = ((hidden_wide - average) * lax.rsqrt(variance + 1e-05) * norm_gain + norm_bias).astype(
        jnp.bfloat16
    )
    frames = (linear(normed, proj_weight) + proj_bias).astype(jnp.bfloat16)
    frame_count = frames.shape[0]
    feature_width = frames.shape[1]
    ranks_total = lax.axis_size("rec")
    slice_rows = centroid_init.shape[0]
    owners_used = (K + slice_rows - 1) // slice_rows
    capacity = max(2, (5 * frame_count + 4 * owners_used - 1) // (4 * owners_used))
    position = lax.axis_index("rec") * frame_count + jnp.arange(frame_count, dtype=jnp.int32)
    is_live = (position < rec_length[0]).astype(jnp.int32)
    frame_index = jnp.arange(frame_count, dtype=jnp.int32)
    earlier = (frame_index[None, :] < frame_index[:, None]).astype(jnp.bfloat16)
    owner_ids = jnp.arange(ranks_total, dtype=jnp.int32)
    cluster_ids = jnp.arange(slice_rows, dtype=jnp.int32)
    frames_wide = frames.astype(jnp.float32)
    centroid = centroid_init
    counts = prior_count
    results = []
    for iteration in range(ITERS):
        chosen = assign[iteration, 0]
        owner_id = chosen // slice_rows
        inner_id = chosen - owner_id * slice_rows
        owner_hot = (owner_id[:, None] == owner_ids[None, :]).astype(jnp.bfloat16)
        before = jnp.dot(earlier, owner_hot, preferred_element_type=jnp.float32)
        slot_id = jnp.sum(before * owner_hot.astype(jnp.float32), axis=1).astype(jnp.int32)
        target = owner_id * capacity + slot_id
        slot_total = ranks_total * capacity
        send_rows = jnp.zeros((slot_total, feature_width), jnp.bfloat16).at[target].set(frames)
        send_ids = jnp.full((slot_total,), -1, jnp.int32).at[target].set(inner_id)
        send_live = jnp.zeros((slot_total,), jnp.int32).at[target].set(is_live)
        got_rows, got_ids, got_live = (
            lax.all_to_all(
                send_rows.reshape(ranks_total, capacity, feature_width),
                "rec",
                split_axis=0,
                concat_axis=0,
                tiled=True,
            ),
            lax.all_to_all(
                send_ids.reshape(ranks_total, capacity),
                "rec",
                split_axis=0,
                concat_axis=0,
                tiled=True,
            ),
            lax.all_to_all(
                send_live.reshape(ranks_total, capacity),
                "rec",
                split_axis=0,
                concat_axis=0,
                tiled=True,
            ),
        )
        got_rows = got_rows.reshape(slot_total, feature_width)
        got_ids = got_ids.reshape(slot_total)
        got_live = got_live.reshape(slot_total)
        member = ((got_ids[:, None] == cluster_ids[None, :]) & (got_live[:, None] > 0)).astype(
            jnp.bfloat16
        )
        partial_value = jnp.dot(member.T, got_rows, preferred_element_type=jnp.float32)
        hit_count = jnp.sum(member.astype(jnp.float32), axis=0)
        coded = centroid.astype(jnp.bfloat16)
        codebook = lax.all_gather(coded, "rec", axis=0, tiled=True)
        picked = jnp.take(codebook, chosen, axis=0).astype(jnp.float32)
        gap_value = frames_wide - picked
        results.append(jnp.sum(gap_value * gap_value, axis=1) / feature_width)
        summed, hit_total = lax.psum((partial_value, hit_count), "grp")
        updated = counts + hit_total
        centroid = (counts[:, None] * centroid + summed) / updated[:, None]
        counts = updated
    distortion = jnp.stack(results, 0)[:, None, :]
    return (distortion, centroid)


def solution(mesh):
    in_specs = (
        P("grp", "rec", None),
        P(None, "grp"),
        P(None, "grp"),
        P(None, "grp"),
        P(),
        P(),
        P(None, "grp"),
        P(),
        P("grp"),
        P(None, "grp", "rec"),
        P("rec", None),
        P("rec"),
    )
    out_specs = (P(None, "grp", "rec"), P("rec", None))
    return jax.shard_map(shards, mesh=mesh, in_specs=in_specs, out_specs=out_specs, check_vma=False)
```

profile of v0, /device:TPU:1, one launch (start us, length us, event | category | flops | bytes accessed | tf_op | source)
XLA Modules:
  0.0 582.5 jit_solution(9825672385246203431)
XLA Ops:
  12.4 18.4 %all-to-all-start.3 = ((s32[128,1,2]{2,1,0:T(1,128)}), s32[128,1,2]{2,1,0:T(1,128)S(1)}, u32[]{:S(2)}, u32[]{:S(2)}) async-start(s32[128,1,2]{2,1,0:T(1,128)} %bitcast.16), calls=%async_computation.3 | async-start | bytes 131072 | tf_op jit(solution)/shard_map/all_to_all | solution.py:95
  31.6 2.8 collective-permute-start
  34.4 15.8 %all_gather.24 = bf16[512,768]{0,1:T(8,128)(2,1)S(1)} all-gather(bf16[512,192]{0,1:T(8,128)(2,1)} %param.20), channel_id=1, replica_groups=mesh['rec'=128,'grp'=4] {'grp'}, dimensions={1}, use_global_device_ids=true | all-gather | bytes 983040 | tf_op jit(solution)/shard_map/all_gather | solution.py:19
  61.2 4.9 fusion.12
  66.3 20.3 %all-gather.9.cloned.1.call-done = bf16[1024,512]{1,0:T(8,128)(2,1)} async-done(((bf16[1024,128]{1,0:T(8,128)(2,1)}), bf16[1024,512]{1,0:T(8,128)(2,1)}) %all-gather.9.cloned.1.call-update) | async-done | bytes 1048592 | tf_op jit(solution)/shard_map/all_gather | solution.py:19
  86.6 2.7 fusion.24
  89.4 15.9 %all-to-all-start.6 = ((s32[128,1,2]{2,1,0:T(1,128)}), s32[128,1,2]{2,1,0:T(1,128)S(1)}, u32[]{:S(2)}, u32[]{:S(2)}) async-start(s32[128,1,2]{2,1,0:T(1,128)} %bitcast.23), calls=%async_computation.6 | async-start | bytes 131072 | tf_op jit(solution)/shard_map/all_to_all | solution.py:95
  105.3 15.1 %all-gather.11.cloned.1.call-done = bf16[1024,512]{1,0:T(8,128)(2,1)} async-done(((bf16[1024,128]{1,0:T(8,128)(2,1)}), bf16[1024,512]{1,0:T(8,128)(2,1)}) %all-gather.11.cloned.1.call-update) | async-done | bytes 1048592 | tf_op jit(solution)/shard_map/all_gather | solution.py:19
  120.4 2.2 convert_reduce_fusion
  122.6 15.9 %all-to-all-start.4 = ((s32[128,1,2]{2,1,0:T(1,128)}), s32[128,1,2]{2,1,0:T(1,128)S(1)}, u32[]{:S(2)}, u32[]{:S(2)}) async-start(s32[128,1,2]{2,1,0:T(1,128)} %bitcast.17), calls=%async_computation.4 | async-start | bytes 131072 | tf_op jit(solution)/shard_map/all_to_all | solution.py:102
  138.5 11.5 %all-to-all-done.4 = s32[128,1,2]{2,1,0:T(1,128)S(1)} async-done(((s32[128,1,2]{2,1,0:T(1,128)}), s32[128,1,2]{2,1,0:T(1,128)S(1)}, u32[]{:S(2)}, u32[]{:S(2)}) %all-to-all-start.4) | async-done | bytes 1056 | tf_op jit(solution)/shard_map/all_to_all | solution.py:102
  150.1 5.6 all-to-all-start.7
  155.9 11.5 %all-to-all-done.7 = s32[128,1,2]{2,1,0:T(1,128)S(1)} async-done(((s32[128,1,2]{2,1,0:T(1,128)}), s32[128,1,2]{2,1,0:T(1,128)S(1)}, u32[]{:S(2)}, u32[]{:S(2)}) %all-to-all-start.7) | async-done | bytes 1056 | tf_op jit(solution)/shard_map/all_to_all | solution.py:102
  167.4 5.7 all-to-all-start
  173.1 11.7 %all-to-all-done = s32[128,1,2]{2,1,0:T(1,128)S(1)} async-done(((s32[128,1,2]{2,1,0:T(1,128)}), s32[128,1,2]{2,1,0:T(1,128)S(1)}, u32[]{:S(2)}, u32[]{:S(2)}) %all-to-all-start) | async-done | bytes 1056 | tf_op jit(solution)/shard_map/all_to_all | solution.py:95
  184.8 5.7 all-to-all-start.1
  193.0 9.1 %all-to-all-done.1 = s32[128,1,2]{2,1,0:T(1,128)S(1)} async-done(((s32[128,1,2]{2,1,0:T(1,128)}), s32[128,1,2]{2,1,0:T(1,128)S(1)}, u32[]{:S(2)}, u32[]{:S(2)}) %all-to-all-start.1) | async-done | bytes 1056 | tf_op jit(solution)/shard_map/all_to_all | solution.py:102
  202.1 5.7 all-to-all-start.5
  210.0 14.8 %all-to-all-done.5 = bf16[128,2,768]{2,1,0:T(2,128)(2,1)S(1)} async-done(((bf16[128,2,768]{2,1,0:T(2,128)(2,1)}), bf16[128,2,768]{2,1,0:T(2,128)(2,1)S(1)}, u32[]{:S(2)}, u32[]{:S(2)}) %all-to-all-start.5) | async-done | bytes 393248 | tf_op jit(solution)/shard_map/all_to_all | solution.py:88
  224.8 7.1 %all-to-all-start.8 = ((bf16[128,2,768]{2,1,0:T(2,128)(2,1)}), bf16[128,2,768]{2,1,0:T(2,128)(2,1)S(1)}, u32[]{:S(2)}, u32[]{:S(2)}) async-start(bf16[128,2,768]{2,1,0:T(2,128)(2,1)} %reshape.452), calls=%async_computation.8 | async-start | bytes 786432 | tf_op jit(solution)/shard_map/all_to_all | solution.py:88
  236.0 1.2 scatter_custom_fusion.2
  238.1 10.7 %all-to-all-done.8 = bf16[128,2,768]{2,1,0:T(2,128)(2,1)S(1)} async-done(((bf16[128,2,768]{2,1,0:T(2,128)(2,1)}), bf16[128,2,768]{2,1,0:T(2,128)(2,1)S(1)}, u32[]{:S(2)}, u32[]{:S(2)}) %all-to-all-start.8) | async-done | bytes 393248 | tf_op jit(solution)/shard_map/all_to_all | solution.py:88
  248.8 7.1 %all-to-all-start.2 = ((bf16[128,2,768]{2,1,0:T(2,128)(2,1)}), bf16[128,2,768]{2,1,0:T(2,128)(2,1)S(1)}, u32[]{:S(2)}, u32[]{:S(2)}) async-start(bf16[128,2,768]{2,1,0:T(2,128)(2,1)} %reshape.448), calls=%async_computation.2 | async-start | bytes 786432 | tf_op jit(solution)/shard_map/all_to_all | solution.py:88
  259.6 13.2 %all-to-all-done.2 = bf16[128,2,768]{2,1,0:T(2,128)(2,1)S(1)} async-done(((bf16[128,2,768]{2,1,0:T(2,128)(2,1)}), bf16[128,2,768]{2,1,0:T(2,128)(2,1)S(1)}, u32[]{:S(2)}, u32[]{:S(2)}) %all-to-all-start.2) | async-done | bytes 393248 | tf_op jit(solution)/shard_map/all_to_all | solution.py:88
  273.8 42.7 %all-reduce.3.cloned.1.call-done = (f32[8]{0:T(128)}, f32[8,768]{1,0:T(8,128)}, f32[8,768]{1,0:T(8,128)}, f32[8]{0:T(128)}, f32[8,768]{1,0:T(8,128)}, /*index=5*/f32[8]{0:T(128)}) async-done(((f32[8]{0:T(128)}, f32[8,768]{1,0:T(8,128)}, f32[8,768]{1,0:T(8,128)}, f32[8]{0:T(128)}, f32[8,768]{1,0:T(8,128)}, /*index=5*/f32[8]{0:T(128)}), (f32[8]{0:T(128)}, f32[8,768]{1,0:T(8,128)}, f32[8,768]{1,0:T(8,128)}, ...) | async-done | bytes 73840 | tf_op jit(solution)/shard_map/psum | solution.py:123
  317.2 1.5 add_divide_fusion
  320.0 85.9 %all-gather.15.cloned.1.call-done = bf16[1024,768]{1,0:T(8,128)(2,1)} async-done(((bf16[8,768]{1,0:T(8,128)(2,1)}), bf16[1024,768]{1,0:T(8,128)(2,1)}) %all-gather.15.cloned.1.call-update) | async-done | bytes 1572880 | tf_op jit(solution)/shard_map/all_gather | solution.py:119
  405.9 2.6 gather_fusion.1
  408.5 80.4 %all-gather.17.cloned.1.call-done = bf16[1024,768]{1,0:T(8,128)(2,1)} async-done(((bf16[8,768]{1,0:T(8,128)(2,1)}), bf16[1024,768]{1,0:T(8,128)(2,1)}) %all-gather.17.cloned.1.call-update) | async-done | bytes 1572880 | tf_op jit(solution)/shard_map/all_gather | solution.py:119
  488.9 2.6 gather_fusion.2
  491.5 80.6 %all-gather.13.cloned.1.call-done = bf16[1024,768]{1,0:T(8,128)(2,1)} async-done(((bf16[8,768]{1,0:T(8,128)(2,1)}), bf16[1024,768]{1,0:T(8,128)(2,1)}) %all-gather.13.cloned.1.call-update) | async-done | bytes 1572880 | tf_op jit(solution)/shard_map/all_gather | solution.py:119
  572.1 2.6 gather_fusion
  (95 shorter events, 33.9 us)
Async XLA Ops:
  7.2 43.7 %copy-start = (bf16[1,1024,512]{2,1,0:T(8,128)(2,1)S(1)}, bf16[1,1024,512]{2,1,0:T(8,128)(2,1)}, u32[]{:S(2)}) copy-start(bf16[1,1024,512]{2,1,0:T(8,128)(2,1)} %param.14) | copy-start | bytes 3145732
  7.2 54.0 %all-gather.7.cloned.1.call-start = ((), (), s32[]{:S(2)}) async-start(), calls=%async_computation.9 | async-start | bytes 1966080 | tf_op jit(solution)/shard_map/all_gather | solution.py:19
  7.9 78.7 %all-gather.9.cloned.1.call-start = ((), (), s32[]{:S(2)}) async-start(), calls=%async_computation.10 | async-start | bytes 1310720 | tf_op jit(solution)/shard_map/all_gather | solution.py:19
  12.4 77.0 %all-to-all-start.3 = ((s32[128,1,2]{2,1,0:T(1,128)}), s32[128,1,2]{2,1,0:T(1,128)S(1)}, u32[]{:S(2)}, u32[]{:S(2)}) async-start(s32[128,1,2]{2,1,0:T(1,128)} %bitcast.16), calls=%async_computation.3 | async-start | bytes 131072 | tf_op jit(solution)/shard_map/all_to_all | solution.py:95
  30.8 89.6 %all-gather.11.cloned.1.call-start = ((), (), s32[]{:S(2)}) async-start(), calls=%async_computation.11 | async-start | bytes 1310720 | tf_op jit(solution)/shard_map/all_gather | solution.py:19
  31.6 29.6 %collective-permute-start = (bf16[1,512]{1,0:T(2,128)(2,1)S(1)}, bf16[1,512]{1,0:T(2,128)(2,1)S(1)}, u32[]{:S(2)}, u32[]{:S(2)}) collective-permute-start(bf16[1,512]{1,0:T(2,128)(2,1)S(1)} %slice_bitcast_fusion), channel_id=1, source_target_pairs={{4,0},{8,4},{12,8},{16,12},{20,16},{24,20},{28,24},{32,28},{36,32}... | collective-permute-start | bytes 3080 | tf_op jit(solution)/shard_map/ppermute | solution.py:13
  89.4 33.2 %all-to-all-start.6 = ((s32[128,1,2]{2,1,0:T(1,128)}), s32[128,1,2]{2,1,0:T(1,128)S(1)}, u32[]{:S(2)}, u32[]{:S(2)}) async-start(s32[128,1,2]{2,1,0:T(1,128)} %bitcast.23), calls=%async_computation.6 | async-start | bytes 131072 | tf_op jit(solution)/shard_map/all_to_all | solution.py:95
  105.3 85.1 %copy-start.4 = (f32[768]{0:T(1024)S(1)}, f32[768]{0:T(1024)}, u32[]{:S(2)}) copy-start(f32[768]{0:T(1024)} %param.21) | copy-start | bytes 9220
  105.3 85.1 %copy-start.5 = (f32[512]{0:T(512)S(1)}, f32[512]{0:T(512)}, u32[]{:S(2)}) copy-start(f32[512]{0:T(512)} %param.19) | copy-start | bytes 6148
  105.3 85.1 %copy-start.6 = (f32[512]{0:T(512)S(1)}, f32[512]{0:T(512)}, u32[]{:S(2)}) copy-start(f32[512]{0:T(512)} %param.18) | copy-start | bytes 6148
  122.6 27.4 %all-to-all-start.4 = ((s32[128,1,2]{2,1,0:T(1,128)}), s32[128,1,2]{2,1,0:T(1,128)S(1)}, u32[]{:S(2)}, u32[]{:S(2)}) async-start(s32[128,1,2]{2,1,0:T(1,128)} %bitcast.17), calls=%async_computation.4 | async-start | bytes 131072 | tf_op jit(solution)/shard_map/all_to_all | solution.py:102
  150.1 17.3 %all-to-all-start.7 = ((s32[128,1,2]{2,1,0:T(1,128)}), s32[128,1,2]{2,1,0:T(1,128)S(1)}, u32[]{:S(2)}, u32[]{:S(2)}) async-start(s32[128,1,2]{2,1,0:T(1,128)} %bitcast.24), calls=%async_computation.7 | async-start | bytes 131072 | tf_op jit(solution)/shard_map/all_to_all | solution.py:102
  167.4 17.4 %all-to-all-start = ((s32[128,1,2]{2,1,0:T(1,128)}), s32[128,1,2]{2,1,0:T(1,128)S(1)}, u32[]{:S(2)}, u32[]{:S(2)}) async-start(s32[128,1,2]{2,1,0:T(1,128)} %bitcast.8), calls=%async_computation | async-start | bytes 131072 | tf_op jit(solution)/shard_map/all_to_all | solution.py:95
  184.8 17.3 %all-to-all-start.1 = ((s32[128,1,2]{2,1,0:T(1,128)}), s32[128,1,2]{2,1,0:T(1,128)S(1)}, u32[]{:S(2)}, u32[]{:S(2)}) async-start(s32[128,1,2]{2,1,0:T(1,128)} %bitcast.10), calls=%async_computation.1 | async-start | bytes 131072 | tf_op jit(solution)/shard_map/all_to_all | solution.py:102
  202.1 22.6 %all-to-all-start.5 = ((bf16[128,2,768]{2,1,0:T(2,128)(2,1)}), bf16[128,2,768]{2,1,0:T(2,128)(2,1)S(1)}, u32[]{:S(2)}, u32[]{:S(2)}) async-start(bf16[128,2,768]{2,1,0:T(2,128)(2,1)} %reshape.450), calls=%async_computation.5 | async-start | bytes 786432 | tf_op jit(solution)/shard_map/all_to_all | solution.py:88
  224.8 24.0 %all-to-all-start.8 = ((bf16[128,2,768]{2,1,0:T(2,128)(2,1)}), bf16[128,2,768]{2,1,0:T(2,128)(2,1)S(1)}, u32[]{:S(2)}, u32[]{:S(2)}) async-start(bf16[128,2,768]{2,1,0:T(2,128)(2,1)} %reshape.452), calls=%async_computation.8 | async-start | bytes 786432 | tf_op jit(solution)/shard_map/all_to_all | solution.py:88
  248.8 24.0 %all-to-all-start.2 = ((bf16[128,2,768]{2,1,0:T(2,128)(2,1)}), bf16[128,2,768]{2,1,0:T(2,128)(2,1)S(1)}, u32[]{:S(2)}, u32[]{:S(2)}) async-start(bf16[128,2,768]{2,1,0:T(2,128)(2,1)} %reshape.448), calls=%async_computation.2 | async-start | bytes 786432 | tf_op jit(solution)/shard_map/all_to_all | solution.py:88
  255.9 60.6 %all-reduce.3.cloned.1.call-start = ((), (), s32[]{:S(2)}) async-start(), calls=%async_computation.15 | async-start | bytes 150528 | tf_op jit(solution)/shard_map/psum | solution.py:123
  257.8 58.7 %copy-start.3 = (f32[8]{0:T(128)S(1)}, f32[8]{0:T(128)}, u32[]{:S(2)}) copy-start(f32[8]{0:T(128)} %param.25) | copy-start | bytes 100
  257.8 59.3 %copy-start.1 = (f32[8,768]{1,0:T(8,128)S(1)}, f32[8,768]{1,0:T(8,128)}, u32[]{:S(2)}) copy-start(f32[8,768]{1,0:T(8,128)} %param.24) | copy-start | bytes 73732
  257.8 62.1 %copy-start.2 = (s32[3,1,128]{2,1,0:T(1,128)S(1)}, s32[3,1,128]{2,1,0:T(1,128)}, u32[]{:S(2)}) copy-start(s32[3,1,128]{2,1,0:T(1,128)} %param.23) | copy-start | bytes 4612
  273.8 132.2 %all-gather.15.cloned.1.call-start = ((), (), s32[]{:S(2)}) async-start(), calls=%async_computation.13 | async-start | bytes 1585152 | tf_op jit(solution)/shard_map/all_gather | solution.py:119
  318.7 170.3 %all-gather.17.cloned.1.call-start = ((), (), s32[]{:S(2)}) async-start(), calls=%async_computation.14 | async-start | bytes 1585152 | tf_op jit(solution)/shard_map/all_gather | solution.py:119
  319.2 252.9 %all-gather.13.cloned.1.call-start = ((), (), s32[]{:S(2)}) async-start(), calls=%async_computation.12 | async-start | bytes 1585152 | tf_op jit(solution)/shard_map/all_gather | solution.py:119
Sparse Core Ops, SparseCore 0:
  10.1 43.5 all-gather.6
  55.7 30.8 all-gather.8
  88.7 31.7 all-gather.10
  273.9 42.5 all-reduce.2
  319.5 86.3 all-gather.14
  409.0 79.8 all-gather.16
  492.1 79.9 all-gather.12
where the time goes:
time: 583 us; the launch traced here: 582 us
  waiting for transfers between devices  410 us (70%)
  starting transfers between devices  90.2 us (15%)
  local copies, waits for them, and re-layouts  29.5 us (5%)
  blocking collectives  15.8 us (3%)
  between operations  15.3 us (3%)
  matrix products  13.1 us (2%)
  other arithmetic  8.61 us (1%)
    all_gather x3, waiting for transfers between devices, shards(): codebook = lax.all_gather(coded, 'rec', axis=0, tiled=True)  247 us
    psum x1, waiting for transfers between devices, shards(): summed, hit_total = lax.psum((partial_value, hit_count), 'grp')  42.7 us
    all_to_all x3, starting transfers between devices, shards(): lax.all_to_all(send_ids.reshape(ranks_total, capacity), 'rec', split_axis...  40 us
    all_to_all x3, waiting for transfers between devices, shards(): lax.all_to_all(send_rows.reshape(ranks_total, capacity, feature_width), '...  38.6 us
    all_gather x3, waiting for transfers between devices, linear(): lax.all_gather(weight, 'grp', axis=1, tiled=True)  35.4 us
    all_to_all x3, waiting for transfers between devices, shards(): lax.all_to_all(send_live.reshape(ranks_total, capacity), 'rec', split_axi...  32.1 us
    all_to_all x3, starting transfers between devices, shards(): lax.all_to_all(send_live.reshape(ranks_total, capacity), 'rec', split_axi...  27.2 us
    all_to_all x3, starting transfers between devices, shards(): lax.all_to_all(send_rows.reshape(ranks_total, capacity, feature_width), '...  19.9 us
  transfers between devices with their start and end apart: 17, of which 13 were waited for; matrix products, arithmetic and copies ran while one was open for 7% of the time, Pallas kernels for 0%

commit v1 on v0

v1 whole, which is shorter than its diff:
```python
import jax
import jax.numpy as jnp
from jax import lax
from jax.experimental import pallas as pl
from jax.experimental.pallas import tpu as pltpu
from jax.sharding import PartitionSpec as P

ITERS = 3
CAP = 2
MESH = pl.DeviceIdType.MESH


def shifted(value, axis, steps):
    count = lax.axis_size(axis)
    initial, last = (max(0, -steps), min(count, count - steps))
    return lax.ppermute(value, axis, [(source, source + steps) for source in range(initial, last)])


def gather_kernel(*refs):
    ins, outs = refs[:4], refs[4:8]
    send, near, cross = refs[8:]
    rec, grp = lax.axis_index("rec"), lax.axis_index("grp")
    core = lax.rem(rec, 2)
    mate = (rec + 1 - 2 * core, grp)
    right = (rec, lax.rem(grp + 1, 4))
    left = (rec, lax.rem(grp + 3, 4))

    barrier = pltpu.get_barrier_semaphore()
    for peer in (left, right, mate):
        pl.semaphore_signal(barrier, inc=1, device_id=peer, device_id_type=MESH)
    pl.semaphore_wait(barrier, 3)

    def rows(w, half, part):
        quarter = ins[w].shape[0] // 4
        return pl.ds(pl.multiple_of((2 * half + part) * quarter, quarter), quarter)

    def place(w, owner, half, part):
        if outs[w].ndim == 3:
            return outs[w].at[owner, rows(w, half, part), :]
        width = ins[w].shape[1]
        return outs[w].at[rows(w, half, part), pl.ds(pl.multiple_of(owner * width, width), width)]

    started = []

    def copy(w, source, target, slot, arrival, peer):
        made = pltpu.make_async_remote_copy(
            src_ref=source, dst_ref=target, send_sem=send.at[w, slot], recv_sem=arrival.at[w, slot % 6],
            device_id=peer, device_id_type=MESH,
        )
        return made

    owner_of = [lax.rem(grp + 3, 4), lax.rem(grp + 3, 4), lax.rem(grp + 1, 4), lax.rem(grp + 1, 4),
                lax.rem(grp + 2, 4), lax.rem(grp + 2, 4)]
    part_of = [0, 1, 1, 0, 0, 1]
    direct = {}
    for w in range(4):
        for slot, peer in ((0, right), (2, left), (1, right), (3, left)):
            part = part_of[slot]
            made = copy(w, ins[w].at[rows(w, core, part), :], place(w, grp, core, part), slot, near, peer)
            made.start()
            direct[w, slot] = made
    for w in range(4):
        if outs[w].ndim == 3:
            outs[w][grp] = ins[w][...]
        else:
            width = ins[w].shape[1]
            outs[w][:, pl.ds(pl.multiple_of(grp * width, width), width)] = ins[w][...]
    relayed, crossed = {}, {}

    def pass_on(w, slot):
        block = place(w, owner_of[slot], core, part_of[slot])
        if slot in (0, 2):
            hop = copy(w, block, block, 4 + slot // 2, near, right if slot == 0 else left)
            hop.start()
            relayed[w, 4 + slot // 2] = hop
        over = copy(w, block, block, 6 + slot, cross, mate)
        over.start()
        crossed[w, slot] = over

    for w in range(4):
        for slot in (0, 2, 1, 3):
            direct[w, slot].wait_recv()
            pass_on(w, slot)
    for w in range(4):
        for slot in (4, 5):
            relayed[w, slot].wait_recv()
            pass_on(w, slot)
    for w in range(4):
        for slot in range(6):
            crossed[w, slot].wait_recv()
            crossed[w, slot].wait_send()
        for made in [direct[w, slot] for slot in range(4)] + [relayed[w, slot] for slot in (4, 5)]:
            made.wait_send()


def gather_weights(w5, w6, w7, wp):
    shapes = [jax.ShapeDtypeStruct((w.shape[0], 4 * w.shape[1]), w.dtype) for w in (w5, w6, w7)]
    shapes.append(jax.ShapeDtypeStruct((4,) + wp.shape, wp.dtype))
    vmem = pl.BlockSpec(memory_space=pltpu.VMEM)
    return pl.pallas_call(
        gather_kernel,
        out_shape=shapes,
        in_specs=[vmem] * 4,
        out_specs=[vmem] * 4,
        scratch_shapes=[
            pltpu.SemaphoreType.DMA((4, 12)),
            pltpu.SemaphoreType.DMA((4, 6)),
            pltpu.SemaphoreType.DMA((4, 6)),
        ],
        compiler_params=pltpu.CompilerParams(
            collective_id=0, has_side_effects=True, vmem_limit_bytes=32 * 1024 * 1024
        ),
    )(w5, w6, w7, wp)


def total_kernel(part_ref, out_ref, held, send, arrive):
    rec, grp = lax.axis_index("rec"), lax.axis_index("grp")
    barrier = pltpu.get_barrier_semaphore()
    for step in (1, 2, 3):
        pl.semaphore_signal(
            barrier, inc=1, device_id=(rec, lax.rem(grp + step, 4)), device_id_type=MESH
        )
    pl.semaphore_wait(barrier, 3)
    copies = []
    for step in (2, 1, 3):
        made = pltpu.make_async_remote_copy(
            src_ref=part_ref, dst_ref=held.at[grp], send_sem=send.at[step - 1],
            recv_sem=arrive.at[step - 1], device_id=(rec, lax.rem(grp + step, 4)), device_id_type=MESH,
        )
        made.start()
        copies.append(made)
    held[grp] = part_ref[...]
    for made in copies:
        made.wait()
    out_ref[...] = (held[0] + held[1]) + (held[2] + held[3])


def grp_total(part):
    vmem = pl.BlockSpec(memory_space=pltpu.VMEM)
    return pl.pallas_call(
        total_kernel,
        out_shape=jax.ShapeDtypeStruct(part.shape, part.dtype),
        in_specs=[vmem],
        out_specs=vmem,
        scratch_shapes=[
            pltpu.VMEM((4,) + part.shape, part.dtype),
            pltpu.SemaphoreType.DMA((3,)),
            pltpu.SemaphoreType.DMA((3,)),
        ],
        compiler_params=pltpu.CompilerParams(collective_id=1, has_side_effects=True),
    )(part)


def linear(inputs, weight):
    return jnp.dot(inputs, weight, preferred_element_type=jnp.float32)


def conv_layer(inputs, weight):
    return jax.nn.gelu(linear(inputs, weight), approximate=False).astype(jnp.bfloat16)


def shards(
    conv_in,
    conv5_weight,
    conv6_weight,
    conv7_weight,
    norm_gain,
    norm_bias,
    proj_weight,
    proj_bias,
    rec_length,
    assign,
    centroid_init,
    prior_count,
):
    w5, w6, w7, wp = gather_weights(conv5_weight, conv6_weight, conv7_weight, proj_weight)
    signal = conv_in[0]
    sample_rows, channels = signal.shape
    next_row = shifted(signal[:1], "rec", -1)
    paired = signal.reshape(sample_rows // 2, 2 * channels)
    trailing = jnp.concatenate([signal[2::2], next_row], 0)
    stacked = jnp.concatenate([paired, trailing], 1)
    hidden = conv_layer(stacked, w5)
    hidden = conv_layer(hidden.reshape(-1, 2 * channels), w6)
    hidden = conv_layer(hidden.reshape(-1, 2 * channels), w7)
    hidden_wide = hidden.astype(jnp.float32)
    average = jnp.mean(hidden_wide, axis=-1, keepdims=True)
    variance = jnp.mean((hidden_wide - average) ** 2, axis=-1, keepdims=True)
    normed = ((hidden_wide - average) * lax.rsqrt(variance + 1e-05) * norm_gain + norm_bias).astype(
        jnp.bfloat16
    )
    projected = jnp.concatenate([linear(normed, wp[g]) for g in range(4)], 1)
    frames = (projected + proj_bias).astype(jnp.bfloat16)
    frame_count, width = frames.shape

    ranks = lax.axis_size("rec")
    slice_rows = centroid_init.shape[0]
    position = lax.axis_index("rec") * frame_count + jnp.arange(frame_count, dtype=jnp.int32)
    is_live = (position < rec_length[0]).astype(jnp.int32)
    frame_index = jnp.arange(frame_count, dtype=jnp.int32)
    earlier = frame_index[None, :] < frame_index[:, None]
    owner_ids = jnp.arange(ranks, dtype=jnp.int32)
    cluster_ids = jnp.arange(slice_rows, dtype=jnp.int32)

    chosen = assign[:, 0]
    owner = chosen // slice_rows
    inner = chosen - owner * slice_rows
    same = owner[:, :, None] == owner[:, None, :]
    slot = jnp.sum((same & earlier[None]).astype(jnp.int32), axis=2)
    tag = (inner + 1) * (2 * is_live - 1)[None, :]
    picks, rows, tags = [], [], []
    for t in range(ITERS):
        for s in range(CAP):
            pick = (owner[t][None, :] == owner_ids[:, None]) & (slot[t] == s)[None, :]
            picks.append(pick)
            rows.append(linear(pick.astype(jnp.bfloat16), frames).astype(jnp.bfloat16))
            tags.append(jnp.sum(jnp.where(pick, tag[t][None, :], 0), axis=1))
    meta = jnp.stack(tags, 1).astype(jnp.bfloat16)
    meta = jnp.pad(meta, ((0, 0), (0, 128 - meta.shape[1])))
    sent = jnp.concatenate(rows + [meta], 1)
    got = lax.all_to_all(sent, "rec", split_axis=0, concat_axis=0, tiled=True)
    got_tag = got[:, ITERS * CAP * width : ITERS * CAP * width + ITERS * CAP].astype(jnp.int32)

    sums, hits, named = [], [], []
    for t in range(ITERS):
        total, count = 0.0, 0.0
        for s in range(CAP):
            j = t * CAP + s
            block = got[:, j * width : (j + 1) * width]
            live = got_tag[:, j][:, None] == cluster_ids[None, :] + 1
            named.append(live | (got_tag[:, j][:, None] == -cluster_ids[None, :] - 1))
            total = total + linear(live.astype(jnp.bfloat16).T, block)
            count = count + jnp.sum(live.astype(jnp.float32), axis=0)
        sums.append(total)
        hits.append(count)
    sums, hits = jnp.concatenate(sums, 0), jnp.concatenate(hits, 0)
    part = jnp.concatenate([sums, jnp.broadcast_to(hits[:, None], (hits.shape[0], 128))], 1)
    part = grp_total(part)
    centroid, counts = centroid_init, prior_count
    back = []
    for t in range(ITERS):
        coded = centroid.astype(jnp.bfloat16)
        for s in range(CAP):
            j = t * CAP + s
            block = got[:, j * width : (j + 1) * width].astype(jnp.float32)
            gap = block - linear(named[j].astype(jnp.bfloat16), coded)
            back.append(jnp.sum(gap * gap, axis=1) / width)
        lot = part[t * slice_rows : (t + 1) * slice_rows]
        updated = counts + lot[:, width]
        centroid = (counts[:, None] * centroid + lot[:, :width]) / updated[:, None]
        counts = updated
    back = jnp.pad(jnp.stack(back, 1), ((0, 0), (0, 128 - ITERS * CAP)))
    back = lax.all_to_all(back, "rec", split_axis=0, concat_axis=0, tiled=True)
    results = []
    for t in range(ITERS):
        one = 0.0
        for s in range(CAP):
            j = t * CAP + s
            one = one + jnp.sum(jnp.where(picks[j], back[:, j][:, None], 0.0), axis=0)
        results.append(one)
    return (jnp.stack(results, 0)[:, None, :], centroid)


def solution(mesh):
    in_specs = (
        P("grp", "rec", None),
        P(None, "grp"),
        P(None, "grp"),
        P(None, "grp"),
        P(),
        P(),
        P(None, "grp"),
        P(),
        P("grp"),
        P(None, "grp", "rec"),
        P("rec", None),
        P("rec"),
    )
    out_specs = (P(None, "grp", "rec"), P("rec", None))
    return jax.shard_map(shards, mesh=mesh, in_specs=in_specs, out_specs=out_specs, check_vma=False)
```

time: 583 us -> 159 us (0.27)
  waiting for transfers between devices: 410 us -> 33.9 us
  starting transfers between devices: 90.2 us -> 21.5 us
  Pallas kernels: 0 us -> 33.7 us
  between operations: 15.3 us -> 1.84 us
  local copies, waits for them, and re-layouts: 29.5 us -> 22.6 us
    all_gather x6 -> x0, waiting for transfers between devices: 282 us -> none  [the longest x3 247 us: shards(): codebook = lax.all_gather(coded, 'rec', axis=0, tiled=True)]
    all_to_all x9 -> x1, starting transfers between devices: 87.1 us -> 12.8 us  [shards(): got = lax.all_to_all(sent, 'rec', split_axis=0, concat_axis=0, tiled=True)]
    all_to_all x9 -> x1, waiting for transfers between devices: 82.5 us -> 33.9 us  [shards(): got = lax.all_to_all(sent, 'rec', split_axis=0, concat_axis=0, tiled=True)]
    psum x1 -> x0, waiting for transfers between devices: 42.7 us -> none  [shards(): summed, hit_total = lax.psum((partial_value, hit_count), 'grp')]
    pallas_call x0 -> x2, Pallas kernels: none -> 33.7 us  [the longest x1 25.4 us: gather_weights(): pl.pallas_call(gather_kernel, out_shape=shapes, in_specs=[vmem] * 4, out_...]
    all_to_all x0 -> x1, blocking collectives: none -> 20.7 us  [shards(): back = lax.all_to_all(back, 'rec', split_axis=0, concat_axis=0, tiled=True)]
    all_gather x1 -> x0, blocking collectives: 15.8 us -> none  [linear(): lax.all_gather(weight, 'grp', axis=1, tiled=True)]
    unnamed x15 -> x34, local copies, waits for them, and re-layouts: 0.61 us -> 11.5 us
  transfers between devices with their start and end apart: 17 -> 2, of which waited for: 13 -> 1; matrix products, arithmetic and copies ran while one was open for 7% -> 5% of each run, Pallas kernels for 0% -> 16%
where the time goes in v1:
time: 159 us; the launch traced here: 158 us
  waiting for transfers between devices  33.9 us (21%)
  Pallas kernels  33.7 us (21%)
  local copies, waits for them, and re-layouts  22.6 us (14%)
  starting transfers between devices  21.5 us (14%)
  blocking collectives  20.7 us (13%)
  matrix products  16.9 us (11%)
  other arithmetic  6.7 us (4%)
  between operations  1.84 us (1%)
    all_to_all x1, waiting for transfers between devices, shards(): got = lax.all_to_all(sent, 'rec', split_axis=0, concat_axis=0, tiled=True)  33.9 us
    pallas_call x1, Pallas kernels, gather_weights(): pl.pallas_call(gather_kernel, out_shape=shapes, in_specs=[vmem] * 4, out_...  25.4 us
    all_to_all x1, blocking collectives, shards(): back = lax.all_to_all(back, 'rec', split_axis=0, concat_axis=0, tiled=True)  20.7 us
    dot_general x25, matrix products, linear(): return jnp.dot(inputs, weight, preferred_element_type=jnp.float32)  16.9 us
    all_to_all x1, starting transfers between devices, shards(): got = lax.all_to_all(sent, 'rec', split_axis=0, concat_axis=0, tiled=True)  12.8 us
    unnamed x34, local copies, waits for them, and re-layouts  11.5 us
    ppermute x1, starting transfers between devices, shifted(): lax.ppermute(value, axis, [(source, source + steps) for source in range(i...  8.73 us
    pallas_call x1, Pallas kernels, grp_total(): pl.pallas_call(total_kernel, out_shape=jax.ShapeDtypeStruct(part.shape, p...  8.3 us
  transfers between devices with their start and end apart: 2, of which 1 were waited for; matrix products, arithmetic and copies ran while one was open for 5% of the time, Pallas kernels for 16%

profile of v1, /device:TPU:1, one launch (start us, length us, event | category | flops | bytes accessed | tf_op | source)
XLA Modules:
  0.0 157.9 jit_solution(8448289091805009097)
XLA Ops:
  0.6 0.7 slice_bitcast_fusion
  1.4 8.7 %collective-permute-start = (bf16[1,512]{1,0:T(2,128)(2,1)S(1)}, bf16[1,512]{1,0:T(2,128)(2,1)S(1)}, u32[]{:S(2)}, u32[]{:S(2)}) collective-permute-start(bf16[1,512]{1,0:T(2,128)(2,1)S(1)} %slice_bitcast_fusion), channel_id=1, source_target_pairs={{4,0},{8,4},{12,8},{16,12},{20,16},{24,20},{28,24},{32,28},{36,32}... | collective-permute-start | bytes 3080 | tf_op jit(solution)/shard_map/ppermute | solution.py:16
  10.8 0.7 and_select_fusion
  11.5 0.7 fusion.135
  12.9 2.3 %reshape_squeeze.3 = bf16[512,1024]{1,0:T(8,128)(2,1)} reshape(bf16[1,1024,512]{2,1,0:T(8,128)(2,1)} %param.12) | data formatting | bytes 2097152 | tf_op jit(solution)/shard_map/reshape;squeeze | solution.py:180
  15.4 3.6 %slice.155 = bf16[511,512]{1,0:T(8,128)(2,1)} slice(bf16[1024,512]{1,0:T(8,128)(2,1)S(1)} %bitcast.134), slice={[2:1024:2], [0:512:1]} | slice | bytes 1046528 | tf_op jit(solution)/shard_map/slice | solution.py:181
  19.2 25.4 %shard_map.131 = (bf16[1536,512]{1,0:T(8,128)(2,1)S(1)}, bf16[1024,512]{1,0:T(8,128)(2,1)S(1)}, bf16[1024,512]{1,0:T(8,128)(2,1)S(1)}, bf16[4,512,192]{2,1,0:T(8,128)(2,1)S(1)}) custom-call(bf16[1536,128]{1,0:T(8,128)(2,1)S(1)} %copy-done, bf16[1024,128]{1,0:T(8,128)(2,1)S(1)} %copy-done.1, bf16[1024,128]{1,0:T(8,128)(2,1)S(1)} %copy-done.2, ...), custom_call_target="tpu_custom_call" | custom-call | tf_op jit(solution)/shard_map/pallas_call | solution.py:100
  44.6 1.0 copy-done.3
  45.6 5.4 %fusion.26 = bf16[512,512]{1,0:T(8,128)(2,1)} fusion(bf16[1536,512]{1,0:T(8,128)(2,1)S(1)} %get-tuple-element.6, bf16[1,512]{1,0:T(2,128)(2,1)S(1)} %collective-permute-done, bf16[511,512]{1,0:T(8,128)(2,1)} %slice.155, bf16[512,1024]{1,0:T(8,128)(2,1)} %reshape_squeeze.3), kind=kOutput, calls=%fused_computation.43 | convolution fusion | flops 827064320 | bytes 3670016 | tf_op jit(solution)/shard_map/dot_general | solution.py:155
  51.0 2.0 %reshape.184 = bf16[256,1024]{1,0:T(8,128)(2,1)} reshape(bf16[512,512]{1,0:T(8,128)(2,1)} %fusion.26) | data formatting | bytes 1048576 | tf_op jit(solution)/shard_map/reshape | solution.py:184
  53.0 2.5 %fusion.38 = bf16[256,512]{1,0:T(8,128)(2,1)S(1)} fusion(bf16[256,1024]{1,0:T(8,128)(2,1)} %reshape.184, bf16[1024,512]{1,0:T(8,128)(2,1)S(1)} %copy-done.4), kind=kOutput, calls=%fused_computation.62 | convolution fusion | flops 276955136 | bytes 1835008 | tf_op jit(solution)/shard_map/dot_general | solution.py:155
  55.6 1.0 convert_reduce_fusion
  56.8 0.3 fusion.62
  57.5 0.3 fusion.58
  59.7 0.5 broadcast.261
  60.2 1.5 reduce.30
  61.7 2.1 %reshape.201 = bf16[128,2,2368]{2,1,0:T(2,128)(2,1)} reshape(bf16[128,4736]{1,0:T(8,128)(2,1)S(1)} %reduce.30) | data formatting | bytes 2424832
  63.8 12.8 %all-to-all-start = ((bf16[128,2,2368]{2,1,0:T(2,128)(2,1)}), bf16[128,2,2368]{2,1,0:T(2,128)(2,1)}, u32[]{:S(2)}, u32[]{:S(2)}) async-start(bf16[128,2,2368]{2,1,0:T(2,128)(2,1)} %reshape.201), calls=%async_computation | async-start | bytes 2490368 | tf_op jit(solution)/shard_map/all_to_all | solution.py:221
  76.6 33.9 %all-to-all-done = bf16[128,2,2368]{2,1,0:T(2,128)(2,1)} async-done(((bf16[128,2,2368]{2,1,0:T(2,128)(2,1)}), bf16[128,2,2368]{2,1,0:T(2,128)(2,1)}, u32[]{:S(2)}, u32[]{:S(2)}) %all-to-all-start) | async-done | bytes 1212448 | tf_op jit(solution)/shard_map/all_to_all | solution.py:221
  110.6 7.4 %reshape.202 = bf16[128,1,4736]{2,1,0:T(2,128)(2,1)S(1)} reshape(bf16[128,2,2368]{2,1,0:T(2,128)(2,1)} %all-to-all-done) | data formatting | bytes 2424832
  120.2 0.6 pad_maximum_fusion.part_ref
  120.8 8.3 %shard_map.132 = f32[24,896]{1,0:T(8,128)} custom-call(f32[24,896]{1,0:T(8,128)} %pad_maximum_fusion.part_ref), custom_call_target="tpu_custom_call" | custom-call | tf_op jit(solution)/shard_map/pallas_call | solution.py:140
  129.1 0.8 slice_reduce_fusion.12
  130.0 1.5 add_divide_fusion
  131.4 1.3 fusion.23
  132.8 1.3 fusion.22
  134.1 0.4 fusion.21
  134.5 0.4 fusion.20
  135.0 0.4 fusion.19
  135.4 0.4 fusion.18
  136.0 20.7 %all_to_all.24 = f32[128,1,128]{2,1,0:T(1,128)S(1)} all-to-all(f32[128,1,128]{2,1,0:T(1,128)S(1)} %copy.43), channel_id=1, replica_groups=mesh['rec'=128,'grp'=4] {'rec'}, dimensions={0} | all-to-all | bytes 131072 | tf_op jit(solution)/shard_map/all_to_all | solution.py:253
  157.4 0.6 copy.44
  (94 shorter events, 6.2 us)
Async XLA Ops:
  0.6 14.6 %copy-start.8 = (bf16[512,192]{0,1:T(8,128)(2,1)S(1)}, bf16[512,192]{0,1:T(8,128)(2,1)}, u32[]{:S(2)}) copy-start(bf16[512,192]{0,1:T(8,128)(2,1)} %param.18) | copy-start | bytes 589828
  1.4 44.2 %collective-permute-start = (bf16[1,512]{1,0:T(2,128)(2,1)S(1)}, bf16[1,512]{1,0:T(2,128)(2,1)S(1)}, u32[]{:S(2)}, u32[]{:S(2)}) collective-permute-start(bf16[1,512]{1,0:T(2,128)(2,1)S(1)} %slice_bitcast_fusion), channel_id=1, source_target_pairs={{4,0},{8,4},{12,8},{16,12},{20,16},{24,20},{28,24},{32,28},{36,32}... | collective-permute-start | bytes 3080 | tf_op jit(solution)/shard_map/ppermute | solution.py:16
  12.9 2.5 %copy-start.7 = (bf16[1,1024,512]{2,1,0:T(8,128)(2,1)S(1)}, bf16[1,1024,512]{2,1,0:T(8,128)(2,1)}, u32[]{:S(2)}) copy-start(bf16[1,1024,512]{2,1,0:T(8,128)(2,1)} %param.12) | copy-start | bytes 3145732
  15.2 4.0 %copy-start = (bf16[1536,128]{1,0:T(8,128)(2,1)S(1)}, bf16[1536,128]{1,0:T(8,128)(2,1)}, u32[]{:S(2)}) copy-start(bf16[1536,128]{1,0:T(8,128)(2,1)} %refs_0_.1) | copy-start | bytes 1179652
  15.2 4.0 %copy-start.1 = (bf16[1024,128]{1,0:T(8,128)(2,1)S(1)}, bf16[1024,128]{1,0:T(8,128)(2,1)}, u32[]{:S(2)}) copy-start(bf16[1024,128]{1,0:T(8,128)(2,1)} %refs_1_.1) | copy-start | bytes 786436
  15.2 4.0 %copy-start.2 = (bf16[1024,128]{1,0:T(8,128)(2,1)S(1)}, bf16[1024,128]{1,0:T(8,128)(2,1)}, u32[]{:S(2)}) copy-start(bf16[1024,128]{1,0:T(8,128)(2,1)} %refs_2_.1) | copy-start | bytes 786436
  44.6 1.0 copy-start.3
  45.6 7.4 %copy-start.4 = (bf16[1024,512]{1,0:T(8,128)(2,1)S(1)}, bf16[1024,512]{1,0:T(8,128)(2,1)}, u32[]{:S(2)}) copy-start(bf16[1024,512]{1,0:T(8,128)(2,1)} %copy-done.3) | copy-start | bytes 3145732
  55.6 1.2 copy-start.12
  55.6 1.2 copy-start.13
  56.8 1.3 copy-start.10
  63.8 46.8 %all-to-all-start = ((bf16[128,2,2368]{2,1,0:T(2,128)(2,1)}), bf16[128,2,2368]{2,1,0:T(2,128)(2,1)}, u32[]{:S(2)}, u32[]{:S(2)}) async-start(bf16[128,2,2368]{2,1,0:T(2,128)(2,1)} %reshape.201), calls=%async_computation | async-start | bytes 2490368 | tf_op jit(solution)/shard_map/all_to_all | solution.py:221
  118.2 1.6 %copy-start.5 = (bf16[128,1,4736]{2,0,1:T(8,128)(2,1)}, bf16[128,1,4736]{2,0,1:T(8,128)(2,1)S(1)}, u32[]{:S(2)}) copy-start(bf16[128,1,4736]{2,0,1:T(8,128)(2,1)S(1)} %copy.71) | copy-start | bytes 3637252
  118.2 11.8 %copy-start.11 = (f32[8]{0:T(128)S(1)}, f32[8]{0:T(128)}, u32[]{:S(2)}) copy-start(f32[8]{0:T(128)} %param.23) | copy-start | bytes 100
  118.2 11.8 %copy-start.9 = (f32[8,768]{1,0:T(8,128)S(1)}, f32[8,768]{1,0:T(8,128)}, u32[]{:S(2)}) copy-start(f32[8,768]{1,0:T(8,128)} %param.22) | copy-start | bytes 73732
  120.0 14.2 %copy-start.6 = (bf16[128,1,4736]{2,0,1:T(8,128)(2,1)S(1)}, bf16[128,1,4736]{2,0,1:T(8,128)(2,1)}, u32[]{:S(2)}) copy-start(bf16[128,1,4736]{2,0,1:T(8,128)(2,1)} %copy-done.5) | copy-start | bytes 3637252

commit v2 on v1

--- a/solution.py
+++ b/solution.py
@@ -113,42 +113,184 @@
     )(w5, w6, w7, wp)
 
 
-def total_kernel(part_ref, out_ref, held, send, arrive):
+PIECES = 40
+
+
+def refresh_kernel(
+    sent, start_ref, prior_ref, back_out, centroid_out,
+    got, onehot, part, held, code, reply, back,
+    go_sem, come_sem, own_sem, part_send, part_come, reply_send, reply_come,
+):
     rec, grp = lax.axis_index("rec"), lax.axis_index("grp")
+    ranks = sent.shape[0]
+    lot = ranks // 8
+    width = start_ref.shape[1]
+    lanes = width // 6
+
+    def peer_of(k):
+        shift = lax.rem(k * 53, ranks)
+        y = lax.rem(rec // 16 + shift // 16, ranks // 16)
+        z = lax.rem(lax.rem(rec // 2, 8) + lax.rem(shift // 2, 8), 8)
+        core = lax.rem(rec + shift, 2)
+        return (y * 8 + z) * 2 + core
+
     barrier = pltpu.get_barrier_semaphore()
+
+    @pl.loop(1, ranks)
+    def _(k):
+        pl.semaphore_signal(barrier, inc=1, device_id=(peer_of(k), grp), device_id_type=MESH)
+
     for step in (1, 2, 3):
         pl.semaphore_signal(
             barrier, inc=1, device_id=(rec, lax.rem(grp + step, 4)), device_id_type=MESH
         )
-    pl.semaphore_wait(barrier, 3)
+    pl.semaphore_wait(barrier, ranks + 2)
+
+    @pl.loop(1, ranks)
+    def _(k):
+        peer = peer_of(k)
+        pltpu.make_async_remote_copy(
+            src_ref=sent.at[peer], dst_ref=got.at[rec], send_sem=go_sem, recv_sem=come_sem,
+            device_id=(peer, grp), device_id_type=MESH,
+        ).start()
+
+    own = pltpu.make_async_copy(sent.at[rec], got.at[rec], own_sem)
+    own.start()
+    own.wait()
+    every = pltpu.make_async_remote_copy(
+        src_ref=sent.at[pl.ds(0, ranks - 1)], dst_ref=got.at[pl.ds(0, ranks - 1)], send_sem=go_sem,
+        recv_sem=come_sem, device_id=(peer_of(1), grp), device_id_type=MESH,
+    )
+    every.wait_recv()
+
+    shape = (lot, PIECES, 128)
+    piece = lax.broadcasted_iota(jnp.int32, shape, 1)
+    lane = lax.broadcasted_iota(jnp.int32, shape, 2)
+    in_row = lane == piece // 6
+    column = (lot, PIECES, 1)
+    piece_column = lax.broadcasted_iota(jnp.int32, column, 1)
+    base = ((piece_column // 12) * 6 + lax.rem(piece_column, 6)) * 8 - 1
+    wide_lane = lax.broadcasted_iota(jnp.int32, (lot, PIECES, 256), 2)
+    contract = (((0,), (0,)), ((), ()))
+    ones = jnp.ones((lot * PIECES, 128), jnp.bfloat16)
+
+    def add_up(c, carry):
+        sums, hits = carry
+        block = got[pl.ds(c * lot, lot)].astype(jnp.float32)
+        meta = jnp.broadcast_to(block[:, 36:37, :], shape)
+        tag = jnp.sum(jnp.where(in_row, meta, 0.0), axis=2, keepdims=True).astype(jnp.int32)
+        spot = jnp.where(tag == 0, -1, base + jnp.abs(tag))
+        hot = jnp.where(wide_lane == spot, 1.0, 0.0)
+        live = jnp.where(tag > 0, hot, 0.0)
+        onehot[pl.ds(pl.multiple_of(c * lot * PIECES, lot * PIECES), lot * PIECES), :] = (
+            hot.reshape(lot * PIECES, 256).astype(jnp.bfloat16)
+        )
+        live = live.reshape(lot * PIECES, 256).astype(jnp.bfloat16)
+        flat = block.reshape(lot * PIECES, 128).astype(jnp.bfloat16)
+        sums = sums + lax.dot_general(live, flat, contract, preferred_element_type=jnp.float32)
+        hits = hits + lax.dot_general(live, ones, contract, preferred_element_type=jnp.float32)
+        return sums, hits
+
+    zero = jnp.zeros((256, 128), jnp.float32)
+    sums, hits = lax.fori_loop(0, 8, add_up, (zero, zero))
+    part[0:144, :] = sums[0:144]
+    for t in range(ITERS):
+        part[144 + 8 * t : 152 + 8 * t, :] = hits[48 * t : 48 * t + 8]
+
     copies = []
     for step in (2, 1, 3):
         made = pltpu.make_async_remote_copy(
-            src_ref=part_ref, dst_ref=held.at[grp], send_sem=send.at[step - 1],
-            recv_sem=arrive.at[step - 1], device_id=(rec, lax.rem(grp + step, 4)), device_id_type=MESH,
+            src_ref=part, dst_ref=held.at[grp], send_sem=part_send.at[step - 1],
+            recv_sem=part_come.at[step - 1], device_id=(rec, lax.rem(grp + step, 4)), device_id_type=MESH,
         )
         made.start()
         copies.append(made)
-    held[grp] = part_ref[...]
+    held[grp] = part[...]
     for made in copies:
         made.wait()
-    out_ref[...] = (held[0] + held[1]) + (held[2] + held[3])
-
-
-def grp_total(part):
+
+    code[144:256, :] = jnp.zeros((112, 128), jnp.float32)
+    for l in range(6):
+        centroid = start_ref[:, l * lanes : (l + 1) * lanes]
+        counts = prior_ref[...]
+        for t in range(ITERS):
+            at = (t * 6 + l) * 8
+            code[at : at + 8, :] = centroid.astype(jnp.bfloat16).astype(jnp.float32)
+            total = (held[0, at : at + 8] + held[1, at : at + 8]) + (
+                held[2, at : at + 8] + held[3, at : at + 8]
+            )
+            at = 144 + 8 * t
+            more = (held[0, at : at + 8] + held[1, at : at + 8]) + (
+                held[2, at : at + 8] + held[3, at : at + 8]
+            )
+            updated = counts + more
+            centroid = (counts * centroid + total) / updated
+            counts = updated
+        centroid_out[:, l * lanes : (l + 1) * lanes] = centroid
+    table = code[...].astype(jnp.bfloat16)
+
+    @pl.loop(0, 8)
+    def _(c):
+        block = got[pl.ds(c * lot, lot)].astype(jnp.float32)
+        hot = onehot[pl.ds(pl.multiple_of(c * lot * PIECES, lot * PIECES), lot * PIECES), :]
+        named = jnp.dot(hot, table, preferred_element_type=jnp.float32).reshape(shape)
+        gap = block - named
+        apart = jnp.sum(gap * gap, axis=2, keepdims=True)
+        spread = jnp.where(in_row, apart, 0.0)
+        reply[pl.ds(c * lot, lot)] = jnp.sum(spread, axis=1, keepdims=True) / width
+
+    @pl.loop(1, ranks)
+    def _(k):
+        peer = peer_of(k)
+        pltpu.make_async_remote_copy(
+            src_ref=reply.at[peer], dst_ref=back.at[rec], send_sem=reply_send, recv_sem=reply_come,
+            device_id=(peer, grp), device_id_type=MESH,
+        ).start()
+
+    own = pltpu.make_async_copy(reply.at[rec], back.at[rec], own_sem)
+    own.start()
+    own.wait()
+    all_back = pltpu.make_async_remote_copy(
+        src_ref=reply.at[pl.ds(0, ranks - 1)], dst_ref=back.at[pl.ds(0, ranks - 1)], send_sem=reply_send,
+        recv_sem=reply_come, device_id=(peer_of(1), grp), device_id_type=MESH,
+    )
+    all_back.wait_recv()
+    back_out[...] = back[...]
+    every.wait_send()
+    all_back.wait_send()
+
+
+def refresh(sent, start, prior):
+    ranks = sent.shape[0]
     vmem = pl.BlockSpec(memory_space=pltpu.VMEM)
     return pl.pallas_call(
-        total_kernel,
-        out_shape=jax.ShapeDtypeStruct(part.shape, part.dtype),
-        in_specs=[vmem],
-        out_specs=vmem,
+        refresh_kernel,
+        out_shape=[
+            jax.ShapeDtypeStruct((ranks, 1, 128), jnp.float32),
+            jax.ShapeDtypeStruct(start.shape, jnp.float32),
+        ],
+        in_specs=[vmem] * 3,
+        out_specs=[vmem] * 2,
         scratch_shapes=[
-            pltpu.VMEM((4,) + part.shape, part.dtype),
+            pltpu.VMEM((ranks, PIECES, 128), jnp.bfloat16),
+            pltpu.VMEM((ranks * PIECES, 256), jnp.bfloat16),
+            pltpu.VMEM((168, 128), jnp.float32),
+            pltpu.VMEM((4, 168, 128), jnp.float32),
+            pltpu.VMEM((256, 128), jnp.float32),
+            pltpu.VMEM((ranks, 1, 128), jnp.float32),
+            pltpu.VMEM((ranks, 1, 128), jnp.float32),
+            pltpu.SemaphoreType.DMA,
+            pltpu.SemaphoreType.DMA,
+            pltpu.SemaphoreType.DMA,
             pltpu.SemaphoreType.DMA((3,)),
             pltpu.SemaphoreType.DMA((3,)),
+            pltpu.SemaphoreType.DMA,
+            pltpu.SemaphoreType.DMA,
         ],
-        compiler_params=pltpu.CompilerParams(collective_id=1, has_side_effects=True),
-    )(part)
+        compiler_params=pltpu.CompilerParams(
+            collective_id=1, has_side_effects=True, vmem_limit_bytes=32 * 1024 * 1024
+        ),
+    )(sent, start, prior)
 
 
 def linear(inputs, weight):
@@ -200,7 +342,6 @@
     frame_index = jnp.arange(frame_count, dtype=jnp.int32)
     earlier = frame_index[None, :] < frame_index[:, None]
     owner_ids = jnp.arange(ranks, dtype=jnp.int32)
-    cluster_ids = jnp.arange(slice_rows, dtype=jnp.int32)
 
     chosen = assign[:, 0]
     owner = chosen // slice_rows
@@ -216,41 +357,11 @@
             rows.append(linear(pick.astype(jnp.bfloat16), frames).astype(jnp.bfloat16))
             tags.append(jnp.sum(jnp.where(pick, tag[t][None, :], 0), axis=1))
     meta = jnp.stack(tags, 1).astype(jnp.bfloat16)
-    meta = jnp.pad(meta, ((0, 0), (0, 128 - meta.shape[1])))
-    sent = jnp.concatenate(rows + [meta], 1)
-    got = lax.all_to_all(sent, "rec", split_axis=0, concat_axis=0, tiled=True)
-    got_tag = got[:, ITERS * CAP * width : ITERS * CAP * width + ITERS * CAP].astype(jnp.int32)
-
-    sums, hits, named = [], [], []
-    for t in range(ITERS):
-        total, count = 0.0, 0.0
-        for s in range(CAP):
-            j = t * CAP + s
-            block = got[:, j * width : (j + 1) * width]
-            live = got_tag[:, j][:, None] == cluster_ids[None, :] + 1
-            named.append(live | (got_tag[:, j][:, None] == -cluster_ids[None, :] - 1))
-            total = total + linear(live.astype(jnp.bfloat16).T, block)
-            count = count + jnp.sum(live.astype(jnp.float32), axis=0)
-        sums.append(total)
-        hits.append(count)
-    sums, hits = jnp.concatenate(sums, 0), jnp.concatenate(hits, 0)
-    part = jnp.concatenate([sums, jnp.broadcast_to(hits[:, None], (hits.shape[0], 128))], 1)
-    part = grp_total(part)
-    centroid, counts = centroid_init, prior_count
-    back = []
-    for t in range(ITERS):
-        coded = centroid.astype(jnp.bfloat16)
-        for s in range(CAP):
-            j = t * CAP + s
-            block = got[:, j * width : (j + 1) * width].astype(jnp.float32)
-            gap = block - linear(named[j].astype(jnp.bfloat16), coded)
-            back.append(jnp.sum(gap * gap, axis=1) / width)
-        lot = part[t * slice_rows : (t + 1) * slice_rows]
-        updated = counts + lot[:, width]
-        centroid = (counts[:, None] * centroid + lot[:, :width]) / updated[:, None]
-        counts = updated
-    back = jnp.pad(jnp.stack(back, 1), ((0, 0), (0, 128 - ITERS * CAP)))
-    back = lax.all_to_all(back, "rec", split_axis=0, concat_axis=0, tiled=True)
+    meta = jnp.pad(meta, ((0, 0), (0, PIECES * 128 - 6 * width - meta.shape[1])))
+    sent = jnp.concatenate(rows + [meta], 1).reshape(ranks, PIECES, 128)
+    prior = jnp.broadcast_to(prior_count[:, None], (slice_rows, 128))
+    back, centroid = refresh(sent, centroid_init, prior)
+    back = back[:, 0]
     results = []
     for t in range(ITERS):
         one = 0.0

time: 159 us -> 134 us (0.84)
  Pallas kernels: 33.7 us -> 97 us
  waiting for transfers between devices: 33.9 us -> 0.01 us
  blocking collectives: 20.7 us -> 0 us
  starting transfers between devices: 21.5 us -> 8.73 us
  local copies, waits for them, and re-layouts: 22.6 us -> 12.4 us
  matrix products: 16.9 us -> 11.4 us
  other arithmetic: 6.7 us -> 2.73 us
    pallas_call x1, Pallas kernels: 8.3 us -> 71.6 us  [refresh(): pl.pallas_call(refresh_kernel, out_shape=[jax.ShapeDtypeStruct((ranks, 1,...]
    all_to_all x1 -> x0, waiting for transfers between devices: 33.9 us -> none  [shards(): got = lax.all_to_all(sent, 'rec', split_axis=0, concat_axis=0, tiled=True)]
    all_to_all x1 -> x0, blocking collectives: 20.7 us -> none  [shards(): back = lax.all_to_all(back, 'rec', split_axis=0, concat_axis=0, tiled=True)]
    all_to_all x1 -> x0, starting transfers between devices: 12.8 us -> none  [shards(): got = lax.all_to_all(sent, 'rec', split_axis=0, concat_axis=0, tiled=True)]
    unnamed x34 -> x29, local copies, waits for them, and re-layouts: 11.5 us -> 3 us
    dot_general x25 -> x13, matrix products: 16.9 us -> 11.4 us  [linear(): return jnp.dot(inputs, weight, preferred_element_type=jnp.float32)]
  transfers between devices with their start and end apart: 2 -> 1, of which waited for: 1 -> 0; matrix products, arithmetic and copies ran while one was open for 5% -> 6% of each run, Pallas kernels for 16% -> 19%
where the time goes in v2:
time: 134 us
  Pallas kernels  97 us (72%)
  local copies, waits for them, and re-layouts  12.4 us (9%)
  matrix products  11.4 us (9%)
  starting transfers between devices  8.73 us (7%)
  other arithmetic  2.73 us (2%)
  between operations  1.7 us (1%)
    pallas_call x1, Pallas kernels, refresh(): pl.pallas_call(refresh_kernel, out_shape=[jax.ShapeDtypeStruct((ranks, 1,...  71.6 us
    pallas_call x1, Pallas kernels, gather_weights(): pl.pallas_call(gather_kernel, out_shape=shapes, in_specs=[vmem] * 4, out_...  25.4 us
    dot_general x13, matrix products, linear(): return jnp.dot(inputs, weight, preferred_element_type=jnp.float32)  11.4 us
    ppermute x1, starting transfers between devices, shifted(): lax.ppermute(value, axis, [(source, source + steps) for source in range(i...  8.73 us
    slice x1, local copies, waits for them, and re-layouts, shards(): trailing = jnp.concatenate([signal[2::2], next_row], 0)  3.62 us
    unnamed x29, local copies, waits for them, and re-layouts  3 us
  transfers between devices with their start and end apart: 1, of which 0 were waited for; matrix products, arithmetic and copies ran while one was open for 6% of the time, Pallas kernels for 19%

profile of v2, /device:TPU:1, one launch (start us, length us, event | category | flops | bytes accessed | tf_op | source)
XLA Modules:
  0.0 133.9 jit_solution(3188892350533527926)
XLA Ops:
  0.6 0.7 slice_bitcast_fusion
  1.4 8.7 %collective-permute-start = (bf16[1,512]{1,0:T(2,128)(2,1)S(1)}, bf16[1,512]{1,0:T(2,128)(2,1)S(1)}, u32[]{:S(2)}, u32[]{:S(2)}) collective-permute-start(bf16[1,512]{1,0:T(2,128)(2,1)S(1)} %slice_bitcast_fusion), channel_id=1, source_target_pairs={{4,0},{8,4},{12,8},{16,12},{20,16},{24,20},{28,24},{32,28},{36,32}... | collective-permute-start | bytes 3080 | tf_op jit(solution)/shard_map/ppermute | solution.py:16
  10.8 0.7 and_select_fusion
  11.5 0.7 fusion.90
  12.2 0.2 convert_reduce_fusion.1
  12.9 2.3 %reshape_squeeze.3 = bf16[512,1024]{1,0:T(8,128)(2,1)} reshape(bf16[1,1024,512]{2,1,0:T(8,128)(2,1)} %param.12) | data formatting | bytes 2097152 | tf_op jit(solution)/shard_map/reshape;squeeze | solution.py:322
  15.4 3.6 %slice.77 = bf16[511,512]{1,0:T(8,128)(2,1)} slice(bf16[1024,512]{1,0:T(8,128)(2,1)S(1)} %bitcast.102), slice={[2:1024:2], [0:512:1]} | slice | bytes 1046528 | tf_op jit(solution)/shard_map/slice | solution.py:323
  19.1 0.1 copy.34
  19.2 25.4 %shard_map.131 = (bf16[1536,512]{1,0:T(8,128)(2,1)S(1)}, bf16[1024,512]{1,0:T(8,128)(2,1)S(1)}, bf16[1024,512]{1,0:T(8,128)(2,1)S(1)}, bf16[4,512,192]{2,1,0:T(8,128)(2,1)S(1)}) custom-call(bf16[1536,128]{1,0:T(8,128)(2,1)S(1)} %copy-done, bf16[1024,128]{1,0:T(8,128)(2,1)S(1)} %copy-done.1, bf16[1024,128]{1,0:T(8,128)(2,1)S(1)} %copy-done.2, ...), custom_call_target="tpu_custom_call" | custom-call | tf_op jit(solution)/shard_map/pallas_call | solution.py:100
  44.6 1.0 copy-done.4
  45.6 5.4 %fusion.14 = bf16[512,512]{1,0:T(8,128)(2,1)} fusion(bf16[1536,512]{1,0:T(8,128)(2,1)S(1)} %get-tuple-element.8, bf16[1,512]{1,0:T(2,128)(2,1)S(1)} %collective-permute-done, bf16[511,512]{1,0:T(8,128)(2,1)} %slice.77, bf16[512,1024]{1,0:T(8,128)(2,1)} %reshape_squeeze.3), kind=kOutput, calls=%fused_computation.21 | convolution fusion | flops 827064320 | bytes 3670016 | tf_op jit(solution)/shard_map/dot_general | solution.py:297
  51.0 2.0 %reshape.113 = bf16[256,1024]{1,0:T(8,128)(2,1)} reshape(bf16[512,512]{1,0:T(8,128)(2,1)} %fusion.14) | data formatting | bytes 1048576 | tf_op jit(solution)/shard_map/reshape | solution.py:326
  53.0 2.5 %fusion.26 = bf16[256,512]{1,0:T(8,128)(2,1)S(1)} fusion(bf16[256,1024]{1,0:T(8,128)(2,1)} %reshape.113, bf16[1024,512]{1,0:T(8,128)(2,1)S(1)} %copy-done.5), kind=kOutput, calls=%fused_computation.40 | convolution fusion | flops 276955136 | bytes 1835008 | tf_op jit(solution)/shard_map/dot_general | solution.py:297
  55.6 1.0 convert_reduce_fusion
  56.6 0.2 fusion.37
  56.8 0.3 fusion.50
  57.2 0.3 fusion.48
  57.5 0.3 fusion.46
  57.8 0.3 fusion.44
  58.1 0.2 fusion.34
  58.3 0.2 fusion.11
  58.5 0.2 fusion.10
  58.7 0.2 fusion.9
  59.0 0.2 fusion.8
  59.2 0.2 fusion.7
  59.4 0.2 fusion.6
  59.7 0.3 copy.38
  60.0 0.4 copy-done.9
  60.4 71.6 %shard_map.132 = (f32[128,1,128]{2,1,0:T(1,128)S(1)}, f32[8,768]{1,0:T(8,128)S(1)}) custom-call(bf16[128,40,128]{2,1,0:T(8,128)(2,1)S(1)} %bitcast.100, f32[8,768]{1,0:T(8,128)S(1)} %copy-done.3, f32[8,128]{1,0:T(8,128)S(1)} %broadcast_in_dim.135.prior_ref), custom_call_target="tpu_custom_call" | custom-call | tf_op jit(solution)/shard_map/pallas_call | solution.py:266
  132.0 0.3 slice_reduce_fusion.4
  132.7 0.6 copy.35
  133.3 0.6 copy.70
  (51 shorter events, 1.2 us)
Async XLA Ops:
  0.6 14.6 %copy-start.7 = (bf16[512,192]{0,1:T(8,128)(2,1)S(1)}, bf16[512,192]{0,1:T(8,128)(2,1)}, u32[]{:S(2)}) copy-start(bf16[512,192]{0,1:T(8,128)(2,1)} %param.18) | copy-start | bytes 589828
  1.4 44.2 %collective-permute-start = (bf16[1,512]{1,0:T(2,128)(2,1)S(1)}, bf16[1,512]{1,0:T(2,128)(2,1)S(1)}, u32[]{:S(2)}, u32[]{:S(2)}) collective-permute-start(bf16[1,512]{1,0:T(2,128)(2,1)S(1)} %slice_bitcast_fusion), channel_id=1, source_target_pairs={{4,0},{8,4},{12,8},{16,12},{20,16},{24,20},{28,24},{32,28},{36,32}... | collective-permute-start | bytes 3080 | tf_op jit(solution)/shard_map/ppermute | solution.py:16
  12.5 2.9 %copy-start.6 = (bf16[1,1024,512]{2,1,0:T(8,128)(2,1)S(1)}, bf16[1,1024,512]{2,1,0:T(8,128)(2,1)}, u32[]{:S(2)}) copy-start(bf16[1,1024,512]{2,1,0:T(8,128)(2,1)} %param.12) | copy-start | bytes 3145732
  12.9 6.3 %copy-start = (bf16[1536,128]{1,0:T(8,128)(2,1)S(1)}, bf16[1536,128]{1,0:T(8,128)(2,1)}, u32[]{:S(2)}) copy-start(bf16[1536,128]{1,0:T(8,128)(2,1)} %refs_0_.1) | copy-start | bytes 1179652
  12.9 6.3 %copy-start.1 = (bf16[1024,128]{1,0:T(8,128)(2,1)S(1)}, bf16[1024,128]{1,0:T(8,128)(2,1)}, u32[]{:S(2)}) copy-start(bf16[1024,128]{1,0:T(8,128)(2,1)} %refs_1_.1) | copy-start | bytes 786436
  12.9 6.3 %copy-start.2 = (bf16[1024,128]{1,0:T(8,128)(2,1)S(1)}, bf16[1024,128]{1,0:T(8,128)(2,1)}, u32[]{:S(2)}) copy-start(bf16[1024,128]{1,0:T(8,128)(2,1)} %refs_2_.1) | copy-start | bytes 786436
  44.6 1.0 copy-start.4
  45.6 7.4 %copy-start.5 = (bf16[1024,512]{1,0:T(8,128)(2,1)S(1)}, bf16[1024,512]{1,0:T(8,128)(2,1)}, u32[]{:S(2)}) copy-start(bf16[1024,512]{1,0:T(8,128)(2,1)} %copy-done.4) | copy-start | bytes 3145732
  55.6 1.2 copy-start.10
  55.6 1.2 copy-start.11
  56.8 1.3 copy-start.8
  59.7 0.7 copy-start.9
  59.7 0.7 copy-start.3

commit v3 on v2

v3 whole, which is shorter than its diff:
```python
import jax
import jax.numpy as jnp
from jax import lax
from jax.experimental import pallas as pl
from jax.experimental.pallas import tpu as pltpu
from jax.sharding import PartitionSpec as P

ITERS = 3
CAP = 2
PIECES = 40
MESH = pl.DeviceIdType.MESH


def whole_kernel(
    x_ref, a5, a6, a7, ap, gain_ref, shift_ref, bias_ref, length_ref, assign_ref, start_ref, prior_ref,
    dist_out, centroid_out,
    o5, o6, o7, op, halo, xf, h5, h6, fr, picked, laid, sent,
    got, onehot, part, held, code, reply, back,
    send, near, cross, halo_send, halo_come,
    go_sem, come_sem, own_sem, part_send, part_come, reply_send, reply_come,
):
    ins, outs = (a5, a6, a7, ap), (o5, o6, o7, op)
    rec, grp = lax.axis_index("rec"), lax.axis_index("grp")
    core = lax.rem(rec, 2)
    mate = (rec + 1 - 2 * core, grp)
    right = (rec, lax.rem(grp + 1, 4))
    left = (rec, lax.rem(grp + 3, 4))
    ranks = sent.shape[0]
    lot = ranks // 8
    width = start_ref.shape[1]
    lanes = width // 6
    steps = x_ref.shape[0]
    frames = steps // 8

    def peer_of(k):
        shift = lax.rem(k * 53, ranks)
        y = lax.rem(rec // 16 + shift // 16, ranks // 16)
        z = lax.rem(lax.rem(rec // 2, 8) + lax.rem(shift // 2, 8), 8)
        across = lax.rem(rec + shift, 2)
        return (y * 8 + z) * 2 + across

    barrier = pltpu.get_barrier_semaphore()
    for step in (1, 2, 3):
        pl.semaphore_signal(
            barrier, inc=1, device_id=(rec, lax.rem(grp + step, 4)), device_id_type=MESH
        )

    @pl.loop(1, ranks)
    def _(k):
        pl.semaphore_signal(barrier, inc=1, device_id=(peer_of(k), grp), device_id_type=MESH)

    pl.semaphore_wait(barrier, ranks + 2)

    next_rows = pltpu.make_async_remote_copy(
        src_ref=x_ref.at[pl.ds(0, 16), :], dst_ref=halo, send_sem=halo_send, recv_sem=halo_come,
        device_id=(lax.rem(rec + ranks - 1, ranks), grp), device_id_type=MESH,
    )
    next_rows.start()

    def rows(w, half, part):
        quarter = ins[w].shape[0] // 4
        return pl.ds(pl.multiple_of((2 * half + part) * quarter, quarter), quarter)

    def place(w, owner, half, part):
        if outs[w].ndim == 3:
            return outs[w].at[owner, rows(w, half, part), :]
        width = ins[w].shape[1]
        return outs[w].at[rows(w, half, part), pl.ds(pl.multiple_of(owner * width, width), width)]

    started = []

    def copy(w, source, target, slot, arrival, peer):
        made = pltpu.make_async_remote_copy(
            src_ref=source, dst_ref=target, send_sem=send.at[w, slot], recv_sem=arrival.at[w, slot % 6],
            device_id=peer, device_id_type=MESH,
        )
        return made

    owner_of = [lax.rem(grp + 3, 4), lax.rem(grp + 3, 4), lax.rem(grp + 1, 4), lax.rem(grp + 1, 4),
                lax.rem(grp + 2, 4), lax.rem(grp + 2, 4)]
    part_of = [0, 1, 1, 0, 0, 1]
    direct = {}
    for w in range(4):
        for slot, peer in ((0, right), (2, left), (1, right), (3, left)):
            side = part_of[slot]
            made = copy(w, ins[w].at[rows(w, core, side), :], place(w, grp, core, side), slot, near, peer)
            made.start()
            direct[w, slot] = made
    for w in range(4):
        if outs[w].ndim == 3:
            outs[w][grp] = ins[w][...]
        else:
            wide = ins[w].shape[1]
            outs[w][:, pl.ds(pl.multiple_of(grp * wide, wide), wide)] = ins[w][...]

    square = (ranks, frames)
    blocks = lax.broadcasted_iota(jnp.int32, square, 0)
    frame_row = lax.broadcasted_iota(jnp.int32, (1, frames), 1)
    lane_row = lax.broadcasted_iota(jnp.int32, (ranks, 128), 1)
    earlier = jnp.where(
        lax.broadcasted_iota(jnp.int32, (frames, frames), 0)
        < lax.broadcasted_iota(jnp.int32, (frames, frames), 1), 1.0, 0.0
    ).astype(jnp.bfloat16)
    sign = jnp.where(rec * frames + frame_row < length_ref[0], 1.0, -1.0)
    meta = jnp.zeros((ranks, 128), jnp.float32)
    for t in range(ITERS):
        chosen = assign_ref[t]
        owner = chosen // 8
        tag = (chosen - owner * 8 + 1).astype(jnp.float32) * sign
        hit = blocks == owner
        before = jnp.dot(
            jnp.where(hit, 1.0, 0.0).astype(jnp.bfloat16), earlier, preferred_element_type=jnp.float32
        )
        for s in range(CAP):
            pick = jnp.where(hit, jnp.where(before == s, 1.0, 0.0), 0.0)
            picked[t * CAP + s] = pick
            label = jnp.sum(pick * tag, axis=1, keepdims=True)
            meta = meta + jnp.where(lane_row == t * CAP + s, label, 0.0)
    laid[pl.ds(36, ranks, stride=PIECES), :] = meta
    for q in range(37, PIECES):
        laid[pl.ds(q, ranks, stride=PIECES), :] = jnp.zeros((ranks, 128), jnp.float32)
    for l in range(x_ref.shape[1] // 128):
        xf[l, 0:steps, :] = x_ref[:, l * 128 : (l + 1) * 128].astype(jnp.float32)

    relayed, crossed = {}, {}

    def pass_on(w, slot):
        block = place(w, owner_of[slot], core, part_of[slot])
        if slot in (0, 2):
            hop = copy(w, block, block, 4 + slot // 2, near, right if slot == 0 else left)
            hop.start()
            relayed[w, 4 + slot // 2] = hop
        over = copy(w, block, block, 6 + slot, cross, mate)
        over.start()
        crossed[w, slot] = over

    for w in range(4):
        for slot in (0, 2, 1, 3):
            direct[w, slot].wait_recv()
            pass_on(w, slot)

    def gelu(v):
        return (0.5 * v * (1.0 + lax.erf(v * 0.7071067811865476))).astype(jnp.bfloat16)

    def dot(a, b):
        return jnp.dot(a, b, preferred_element_type=jnp.float32)

    channels = x_ref.shape[1]

    def layer5():
        next_rows.wait_recv()
        last = jnp.where(rec == ranks - 1, 0.0, 1.0)
        store(xf, steps, halo[...].astype(jnp.float32)[0:8] * last)
        for c in range(2):
            base = c * (steps // 2)
            total = jnp.zeros((steps // 4, channels), jnp.float32)
            for tap in range(3):
                rows_in = strided(xf, base + tap, steps // 4)
                total = total + dot(rows_in, o5[tap * channels : (tap + 1) * channels, :])
            store(h5, c * (steps // 4), gelu(total))

    def strided(ref, start, count):
        parts = [ref[l, pl.ds(start, count, stride=2), :] for l in range(channels // 128)]
        return jnp.concatenate(parts, 1).astype(jnp.bfloat16)

    def store(ref, start, value):
        value = value.astype(jnp.float32)
        for l in range(channels // 128):
            ref[l, start : start + value.shape[0], :] = value[:, l * 128 : (l + 1) * 128]

    def layer6():
        count = steps // 4
        store(h6, 0, gelu(dot(strided(h5, 0, count), o6[0:channels, :])
                          + dot(strided(h5, 1, count), o6[channels : 2 * channels, :])))

    def layer7():
        hidden = gelu(dot(strided(h6, 0, frames), o7[0:channels, :])
                      + dot(strided(h6, 1, frames), o7[channels : 2 * channels, :])).astype(jnp.float32)
        average = jnp.mean(hidden, axis=1, keepdims=True)
        away = hidden - average
        variance = jnp.mean(away * away, axis=1, keepdims=True)
        normed = away * lax.rsqrt(variance + 1e-05) * gain_ref[...] + shift_ref[...]
        store(h5, 0, normed)

    def project():
        normed = jnp.concatenate([h5[l, 0:frames, :] for l in range(channels // 128)], 1).astype(jnp.bfloat16)
        pieces = [dot(normed, op[owner]) for owner in range(4)]
        fr[...] = (jnp.concatenate(pieces, 1) + bias_ref[...]).astype(jnp.bfloat16)

    stages = (layer5, layer6, layer7, project)

    def finish(w):
        for slot in range(6):
            crossed[w, slot].wait_recv()
        stages[w]()

    for w in range(4):
        for slot in (4, 5):
            relayed[w, slot].wait_recv()
            pass_on(w, slot)
        if w >= 1:
            finish(w - 1)
    finish(3)
    for j in range(ITERS * CAP):
        rows_out = dot(picked[j].astype(jnp.bfloat16), fr[...])
        for l in range(6):
            laid[pl.ds(j * 6 + l, ranks, stride=PIECES), :] = rows_out[:, l * lanes : (l + 1) * lanes]

    @pl.loop(0, 8)
    def _(c):
        flat = laid[pl.ds(pl.multiple_of(c * lot * PIECES, lot * PIECES), lot * PIECES), :]
        sent[pl.ds(c * lot, lot)] = flat.reshape(lot, PIECES, 128).astype(jnp.bfloat16)

    @pl.loop(1, ranks)
    def _(k):
        peer = peer_of(k)
        pltpu.make_async_remote_copy(
            src_ref=sent.at[peer], dst_ref=got.at[rec], send_sem=go_sem, recv_sem=come_sem,
            device_id=(peer, grp), device_id_type=MESH,
        ).start()

    own = pltpu.make_async_copy(sent.at[rec], got.at[rec], own_sem)
    own.start()
    own.wait()
    every = pltpu.make_async_remote_copy(
        src_ref=sent.at[pl.ds(0, ranks - 1)], dst_ref=got.at[pl.ds(0, ranks - 1)], send_sem=go_sem,
        recv_sem=come_sem, device_id=(peer_of(1), grp), device_id_type=MESH,
    )
    every.wait_recv()

    shape = (lot, PIECES, 128)
    piece = lax.broadcasted_iota(jnp.int32, shape, 1)
    lane = lax.broadcasted_iota(jnp.int32, shape, 2)
    in_row = lane == piece // 6
    column = (lot, PIECES, 1)
    piece_column = lax.broadcasted_iota(jnp.int32, column, 1)
    base = ((piece_column // 12) * 6 + lax.rem(piece_column, 6)) * 8 - 1
    wide_lane = lax.broadcasted_iota(jnp.int32, (lot, PIECES, 256), 2)
    contract = (((0,), (0,)), ((), ()))
    ones = jnp.ones((lot * PIECES, 128), jnp.bfloat16)

    def add_up(c, carry):
        sums, hits = carry
        block = got[pl.ds(c * lot, lot)].astype(jnp.float32)
        meta = jnp.broadcast_to(block[:, 36:37, :], shape)
        tag = jnp.sum(jnp.where(in_row, meta, 0.0), axis=2, keepdims=True).astype(jnp.int32)
        spot = jnp.where(tag == 0, -1, base + jnp.abs(tag))
        hot = jnp.where(wide_lane == spot, 1.0, 0.0)
        live = jnp.where(tag > 0, hot, 0.0)
        onehot[pl.ds(pl.multiple_of(c * lot * PIECES, lot * PIECES), lot * PIECES), :] = (
            hot.reshape(lot * PIECES, 256).astype(jnp.bfloat16)
        )
        live = live.reshape(lot * PIECES, 256).astype(jnp.bfloat16)
        flat = block.reshape(lot * PIECES, 128).astype(jnp.bfloat16)
        sums = sums + lax.dot_general(live, flat, contract, preferred_element_type=jnp.float32)
        hits = hits + lax.dot_general(live, ones, contract, preferred_element_type=jnp.float32)
        return sums, hits

    zero = jnp.zeros((256, 128), jnp.float32)
    sums, hits = lax.fori_loop(0, 8, add_up, (zero, zero))
    part[0:144, :] = sums[0:144]
    for t in range(ITERS):
        part[144 + 8 * t : 152 + 8 * t, :] = hits[48 * t : 48 * t + 8]

    copies = []
    for step in (2, 1, 3):
        made = pltpu.make_async_remote_copy(
            src_ref=part, dst_ref=held.at[grp], send_sem=part_send.at[step - 1],
            recv_sem=part_come.at[step - 1], device_id=(rec, lax.rem(grp + step, 4)), device_id_type=MESH,
        )
        made.start()
        copies.append(made)
    held[grp] = part[...]
    for made in copies:
        made.wait()

    code[144:256, :] = jnp.zeros((112, 128), jnp.float32)
    for l in range(6):
        centroid = start_ref[:, l * lanes : (l + 1) * lanes]
        counts = prior_ref[...]
        for t in range(ITERS):
            at = (t * 6 + l) * 8
            code[at : at + 8, :] = centroid.astype(jnp.bfloat16).astype(jnp.float32)
            total = (held[0, at : at + 8] + held[1, at : at + 8]) + (
                held[2, at : at + 8] + held[3, at : at + 8]
            )
            at = 144 + 8 * t
            more = (held[0, at : at + 8] + held[1, at : at + 8]) + (
                held[2, at : at + 8] + held[3, at : at + 8]
            )
            updated = counts + more
            centroid = (counts * centroid + total) / updated
            counts = updated
        centroid_out[:, l * lanes : (l + 1) * lanes] = centroid
    table = code[...].astype(jnp.bfloat16)

    @pl.loop(0, 8)
    def _(c):
        block = got[pl.ds(c * lot, lot)].astype(jnp.float32)
        hot = onehot[pl.ds(pl.multiple_of(c * lot * PIECES, lot * PIECES), lot * PIECES), :]
        named = jnp.dot(hot, table, preferred_element_type=jnp.float32).reshape(shape)
        gap = block - named
        apart = jnp.sum(gap * gap, axis=2, keepdims=True)
        spread = jnp.where(in_row, apart, 0.0)
        reply[pl.ds(c * lot, lot)] = jnp.sum(spread, axis=1, keepdims=True) / width

    @pl.loop(1, ranks)
    def _(k):
        peer = peer_of(k)
        pltpu.make_async_remote_copy(
            src_ref=reply.at[peer], dst_ref=back.at[rec], send_sem=reply_send, recv_sem=reply_come,
            device_id=(peer, grp), device_id_type=MESH,
        ).start()

    own = pltpu.make_async_copy(reply.at[rec], back.at[rec], own_sem)
    own.start()
    own.wait()
    all_back = pltpu.make_async_remote_copy(
        src_ref=reply.at[pl.ds(0, ranks - 1)], dst_ref=back.at[pl.ds(0, ranks - 1)], send_sem=reply_send,
        recv_sem=reply_come, device_id=(peer_of(1), grp), device_id_type=MESH,
    )
    all_back.wait_recv()
    replies = back[...].reshape(ranks, 128)
    for t in range(ITERS):
        one = jnp.zeros((1, frames), jnp.float32)
        for s in range(CAP):
            j = t * CAP + s
            one = one + jnp.sum(picked[j] * replies[:, j : j + 1], axis=0, keepdims=True)
        dist_out[t] = one
    next_rows.wait_send()
    for w in range(4):
        for slot in range(6):
            crossed[w, slot].wait_send()
        for made in [direct[w, slot] for slot in range(4)] + [relayed[w, slot] for slot in (4, 5)]:
            made.wait_send()
    every.wait_send()
    all_back.wait_send()


def shards(
    conv_in,
    conv5_weight,
    conv6_weight,
    conv7_weight,
    norm_gain,
    norm_bias,
    proj_weight,
    proj_bias,
    rec_length,
    assign,
    centroid_init,
    prior_count,
):
    ranks = lax.axis_size("rec")
    signal = conv_in[0]
    steps, channels = signal.shape
    frames = steps // 8
    slots, width = centroid_init.shape
    prior = jnp.broadcast_to(prior_count[:, None], (slots, 128))
    vmem = pl.BlockSpec(memory_space=pltpu.VMEM)
    smem = pl.BlockSpec(memory_space=pltpu.SMEM)
    bf16, f32, dma = jnp.bfloat16, jnp.float32, pltpu.SemaphoreType.DMA
    return pl.pallas_call(
        whole_kernel,
        out_shape=[
            jax.ShapeDtypeStruct(assign.shape, f32),
            jax.ShapeDtypeStruct(centroid_init.shape, f32),
        ],
        in_specs=[vmem] * 8 + [smem] + [vmem] * 3,
        out_specs=[vmem] * 2,
        scratch_shapes=[
            pltpu.VMEM((3 * channels, channels), bf16),
            pltpu.VMEM((2 * channels, channels), bf16),
            pltpu.VMEM((2 * channels, channels), bf16),
            pltpu.VMEM((4,) + proj_weight.shape, bf16),
            pltpu.VMEM((16, channels), bf16),
            pltpu.VMEM((channels // 128, steps + 8, 128), f32),
            pltpu.VMEM((channels // 128, steps // 2, 128), f32),
            pltpu.VMEM((channels // 128, steps // 4, 128), f32),
            pltpu.VMEM((frames, width), bf16),
            pltpu.VMEM((ITERS * CAP, ranks, frames), f32),
            pltpu.VMEM((ranks * PIECES, 128), f32),
            pltpu.VMEM((ranks, PIECES, 128), bf16),
            pltpu.VMEM((ranks, PIECES, 128), bf16),
            pltpu.VMEM((ranks * PIECES, 256), bf16),
            pltpu.VMEM((168, 128), f32),
            pltpu.VMEM((4, 168, 128), f32),
            pltpu.VMEM((256, 128), f32),
            pltpu.VMEM((ranks, 1, 128), f32),
            pltpu.VMEM((ranks, 1, 128), f32),
            dma((4, 12)), dma((4, 6)), dma((4, 6)), dma, dma,
            dma, dma, dma, dma((3,)), dma((3,)), dma, dma,
        ],
        compiler_params=pltpu.CompilerParams(
            collective_id=0, has_side_effects=True, vmem_limit_bytes=48 * 1024 * 1024
        ),
    )(
        signal, conv5_weight, conv6_weight, conv7_weight, proj_weight, norm_gain[None], norm_bias[None],
        proj_bias[None], rec_length, assign, centroid_init, prior,
    )


def solution(mesh):
    in_specs = (
        P("grp", "rec", None),
        P(None, "grp"),
        P(None, "grp"),
        P(None, "grp"),
        P(),
        P(),
        P(None, "grp"),
        P(),
        P("grp"),
        P(None, "grp", "rec"),
        P("rec", None),
        P("rec"),
    )
    out_specs = (P(None, "grp", "rec"), P("rec", None))
    return jax.shard_map(shards, mesh=mesh, in_specs=in_specs, out_specs=out_specs, check_vma=False)
```

time: 134 us -> 111 us (0.83)
  matrix products: 11.4 us -> 0 us
  starting transfers between devices: 8.73 us -> 0 us
  local copies, waits for them, and re-layouts: 12.4 us -> 6.15 us
  Pallas kernels: 97 us -> 103 us
  other arithmetic: 2.73 us -> 0 us
    dot_general x13 -> x0, matrix products: 11.4 us -> none  [linear(): return jnp.dot(inputs, weight, preferred_element_type=jnp.float32)]
    ppermute x1 -> x0, starting transfers between devices: 8.73 us -> none  [shifted(): lax.ppermute(value, axis, [(source, source + steps) for source in range(i...]
    pallas_call x2 -> x1, Pallas kernels: 97 us -> 103 us  [shards(): pl.pallas_call(whole_kernel, out_shape=[jax.ShapeDtypeStruct(assign.shape...]
    slice x3 -> x0, local copies, waits for them, and re-layouts: 4.66 us -> none  [the longest x1 3.62 us: shards(): trailing = jnp.concatenate([signal[2::2], next_row], 0)]
    another operation x3 -> x0, local copies, waits for them, and re-layouts: 2.5 us -> none  [the longest x1 2.33 us: shards(): paired = signal.reshape(sample_rows // 2, 2 * channels)]
    unnamed x29 -> x21, local copies, waits for them, and re-layouts: 3 us -> 5.42 us
    reshape x2 -> x0, local copies, waits for them, and re-layouts: 2.12 us -> none  [the longest x1 2.03 us: shards(): hidden = conv_layer(hidden.reshape(-1, 2 * channels), w6)]
  transfers between devices with their start and end apart: 1 -> 0, of which waited for: 0 -> 0; matrix products, arithmetic and copies ran while one was open for 6% -> 0% of each run, Pallas kernels for 19% -> 0%
where the time goes in v3:
time: 111 us; the launch traced here: 110 us
  Pallas kernels  103 us (93%)
  local copies, waits for them, and re-layouts  6.15 us (6%)
  between operations  1.43 us (1%)
    pallas_call x1, Pallas kernels, shards(): pl.pallas_call(whole_kernel, out_shape=[jax.ShapeDtypeStruct(assign.shape...  103 us
    unnamed x21, local copies, waits for them, and re-layouts  5.42 us

profile of v3, /device:TPU:1, one launch (start us, length us, event | category | flops | bytes accessed | tf_op | source)
XLA Modules:
  0.0 110.5 jit_solution(2841649063565377897)
XLA Ops:
  0.6 0.0 copy-start.8
  0.6 0.0 copy-start.1
  1.3 0.0 copy-done.8
  1.4 0.7 broadcast_in_dim.18.prior_ref
  2.1 0.0 copy-start.4
  2.1 0.0 copy-start.5
  2.1 0.0 copy-start.6
  2.1 0.0 copy-start.7
  2.1 1.1 %copy.14.ap = bf16[512,192]{1,0:T(8,128)(2,1)S(1)} copy(bf16[512,192]{0,1:T(8,128)(2,1)} %param.18) | data formatting | bytes 393216 | tf_op args[6]
  3.2 0.0 copy-done.1
  3.2 0.0 copy-done.4
  3.2 0.0 copy-done.5
  3.3 0.0 copy-done.6
  3.3 0.0 copy-done.7
  3.3 0.0 copy-start
  3.3 1.2 %copy-done = bf16[1,1024,512]{2,1,0:T(8,128)(2,1)S(1)} copy-done((bf16[1,1024,512]{2,1,0:T(8,128)(2,1)S(1)}, bf16[1,1024,512]{2,1,0:T(8,128)(2,1)}, u32[]{:S(2)}) %copy-start) | copy-done | bytes 1048600
  4.5 0.0 copy-start.2
  4.5 0.9 copy-done.2
  5.5 0.0 copy-start.3
  5.5 0.9 copy-done.3
  6.4 102.9 %shard_map.131 = (f32[3,1,128]{2,1,0:T(1,128)S(1)}, f32[8,768]{1,0:T(8,128)S(1)}) custom-call(bf16[1024,512]{1,0:T(8,128)(2,1)S(1)} %bitcast.3, bf16[1536,128]{1,0:T(8,128)(2,1)S(1)} %copy-done.1, bf16[1024,128]{1,0:T(8,128)(2,1)S(1)} %copy-done.2, bf16[1024,128]{1,0:T(8,128)(2,1)S(1)} %copy-done.3, bf16[512,192]{1,0:T(8,128)(2,1)S(1)} %copy.14.ap, ...), custom_call_target="tpu_custom_call" | custom-call | tf_op jit(solution)/shard_map/pallas_call | solution.py:363
  109.3 0.6 copy.18
  109.9 0.6 copy.19
  (1 shorter events, 0.0 us)
Async XLA Ops:
  0.6 0.7 copy-start.8
  0.6 2.6 %copy-start.1 = (bf16[1536,128]{1,0:T(8,128)(2,1)S(1)}, bf16[1536,128]{1,0:T(8,128)(2,1)}, u32[]{:S(2)}) copy-start(bf16[1536,128]{1,0:T(8,128)(2,1)} %a5.1) | copy-start | bytes 1179652
  2.1 1.1 %copy-start.4 = (f32[8,768]{1,0:T(8,128)S(1)}, f32[8,768]{1,0:T(8,128)}, u32[]{:S(2)}) copy-start(f32[8,768]{1,0:T(8,128)} %start_ref.1) | copy-start | bytes 73732
  2.1 1.1 %copy-start.5 = (f32[512]{0:T(512)S(1)}, f32[512]{0:T(512)}, u32[]{:S(2)}) copy-start(f32[512]{0:T(512)} %param.16) | copy-start | bytes 6148
  2.1 1.2 %copy-start.6 = (f32[512]{0:T(512)S(1)}, f32[512]{0:T(512)}, u32[]{:S(2)}) copy-start(f32[512]{0:T(512)} %param.17) | copy-start | bytes 6148
  2.1 1.2 %copy-start.7 = (s32[3,1,128]{2,1,0:T(1,128)S(1)}, s32[3,1,128]{2,1,0:T(1,128)}, u32[]{:S(2)}) copy-start(s32[3,1,128]{2,1,0:T(1,128)} %assign_ref.1) | copy-start | bytes 4612
  3.3 1.2 %copy-start = (bf16[1,1024,512]{2,1,0:T(8,128)(2,1)S(1)}, bf16[1,1024,512]{2,1,0:T(8,128)(2,1)}, u32[]{:S(2)}) copy-start(bf16[1,1024,512]{2,1,0:T(8,128)(2,1)} %param.12) | copy-start | bytes 3145732
  4.5 0.9 copy-start.2
  5.5 0.9 copy-start.3

commit v4 on v3

--- a/solution.py
+++ b/solution.py
@@ -14,9 +14,9 @@
 def whole_kernel(
     x_ref, a5, a6, a7, ap, gain_ref, shift_ref, bias_ref, length_ref, assign_ref, start_ref, prior_ref,
     dist_out, centroid_out,
-    o5, o6, o7, op, halo, xf, h5, h6, fr, picked, laid, sent,
+    o5, o6, o7, op, halo, xv, xf, h5, h6, fr, picked, laid, sent,
     got, onehot, part, held, code, reply, back,
-    send, near, cross, halo_send, halo_come,
+    send, near, cross, load_sem, halo_send, halo_come,
     go_sem, come_sem, own_sem, part_send, part_come, reply_send, reply_come,
 ):
     ins, outs = (a5, a6, a7, ap), (o5, o6, o7, op)
@@ -32,12 +32,23 @@
     steps = x_ref.shape[0]
     frames = steps // 8
 
-    def peer_of(k):
-        shift = lax.rem(k * 53, ranks)
-        y = lax.rem(rec // 16 + shift // 16, ranks // 16)
-        z = lax.rem(lax.rem(rec // 2, 8) + lax.rem(shift // 2, 8), 8)
-        across = lax.rem(rec + shift, 2)
-        return (y * 8 + z) * 2 + across
+    across = (core, 1 - core)
+    depth = [lax.rem(lax.div(rec, 2) + dz, 8) * 2 for dz in range(8)]
+    level = lax.div(rec, 16)
+
+    def for_peers(act):
+        def turn(i, skip):
+            for dz in range(8):
+                base = lax.rem(level + i + dz, 8) * 16 + depth[dz]
+                for dc in range(2):
+                    if not (skip and dz == 0 and dc == 0):
+                        act(base + across[dc])
+
+        turn(0, True)
+
+        @pl.loop(1, ranks // 16)
+        def _(i):
+            turn(i, False)
 
     barrier = pltpu.get_barrier_semaphore()
     for step in (1, 2, 3):
@@ -45,9 +56,12 @@
             barrier, inc=1, device_id=(rec, lax.rem(grp + step, 4)), device_id_type=MESH
         )
 
-    @pl.loop(1, ranks)
-    def _(k):
-        pl.semaphore_signal(barrier, inc=1, device_id=(peer_of(k), grp), device_id_type=MESH)
+    @for_peers
+    def _(peer):
+        pl.semaphore_signal(barrier, inc=1, device_id=(peer, grp), device_id_type=MESH)
+
+    load = pltpu.make_async_copy(x_ref, xv, load_sem.at[4])
+    load.start()
 
     pl.semaphore_wait(barrier, ranks + 2)
 
@@ -86,12 +100,12 @@
             made = copy(w, ins[w].at[rows(w, core, side), :], place(w, grp, core, side), slot, near, peer)
             made.start()
             direct[w, slot] = made
+    loads = []
     for w in range(4):
-        if outs[w].ndim == 3:
-            outs[w][grp] = ins[w][...]
-        else:
-            wide = ins[w].shape[1]
-            outs[w][:, pl.ds(pl.multiple_of(grp * wide, wide), wide)] = ins[w][...]
+        wide = ins[w].shape[1]
+        kept = outs[w].at[grp] if w == 3 else outs[w].at[:, pl.ds(pl.multiple_of(grp * wide, wide), wide)]
+        loads.append(pltpu.make_async_copy(ins[w], kept, load_sem.at[w]))
+        loads[w].start()
 
     square = (ranks, frames)
     blocks = lax.broadcasted_iota(jnp.int32, square, 0)
@@ -119,8 +133,9 @@
     laid[pl.ds(36, ranks, stride=PIECES), :] = meta
     for q in range(37, PIECES):
         laid[pl.ds(q, ranks, stride=PIECES), :] = jnp.zeros((ranks, 128), jnp.float32)
+    load.wait()
     for l in range(x_ref.shape[1] // 128):
-        xf[l, 0:steps, :] = x_ref[:, l * 128 : (l + 1) * 128].astype(jnp.float32)
+        xf[l, 0:steps, :] = xv[:, l * 128 : (l + 1) * 128].astype(jnp.float32)
 
     relayed, crossed = {}, {}
 
@@ -184,7 +199,10 @@
 
     def project():
         normed = jnp.concatenate([h5[l, 0:frames, :] for l in range(channels // 128)], 1).astype(jnp.bfloat16)
-        pieces = [dot(normed, op[owner]) for owner in range(4)]
+        pieces = [
+            lax.dot_general(normed, op[owner], (((1,), (1,)), ((), ())), preferred_element_type=jnp.float32)
+            for owner in range(4)
+        ]
         fr[...] = (jnp.concatenate(pieces, 1) + bias_ref[...]).astype(jnp.bfloat16)
 
     stages = (layer5, layer6, layer7, project)
@@ -192,6 +210,7 @@
     def finish(w):
         for slot in range(6):
             crossed[w, slot].wait_recv()
+        loads[w].wait()
         stages[w]()
 
     for w in range(4):
@@ -211,9 +230,8 @@
         flat = laid[pl.ds(pl.multiple_of(c * lot * PIECES, lot * PIECES), lot * PIECES), :]
         sent[pl.ds(c * lot, lot)] = flat.reshape(lot, PIECES, 128).astype(jnp.bfloat16)
 
-    @pl.loop(1, ranks)
-    def _(k):
-        peer = peer_of(k)
+    @for_peers
+    def _(peer):
         pltpu.make_async_remote_copy(
             src_ref=sent.at[peer], dst_ref=got.at[rec], send_sem=go_sem, recv_sem=come_sem,
             device_id=(peer, grp), device_id_type=MESH,
@@ -224,7 +242,7 @@
     own.wait()
     every = pltpu.make_async_remote_copy(
         src_ref=sent.at[pl.ds(0, ranks - 1)], dst_ref=got.at[pl.ds(0, ranks - 1)], send_sem=go_sem,
-        recv_sem=come_sem, device_id=(peer_of(1), grp), device_id_type=MESH,
+        recv_sem=come_sem, device_id=mate, device_id_type=MESH,
     )
     every.wait_recv()
 
@@ -304,9 +322,8 @@
         spread = jnp.where(in_row, apart, 0.0)
         reply[pl.ds(c * lot, lot)] = jnp.sum(spread, axis=1, keepdims=True) / width
 
-    @pl.loop(1, ranks)
-    def _(k):
-        peer = peer_of(k)
+    @for_peers
+    def _(peer):
         pltpu.make_async_remote_copy(
             src_ref=reply.at[peer], dst_ref=back.at[rec], send_sem=reply_send, recv_sem=reply_come,
             device_id=(peer, grp), device_id_type=MESH,
@@ -317,7 +334,7 @@
     own.wait()
     all_back = pltpu.make_async_remote_copy(
         src_ref=reply.at[pl.ds(0, ranks - 1)], dst_ref=back.at[pl.ds(0, ranks - 1)], send_sem=reply_send,
-        recv_sem=reply_come, device_id=(peer_of(1), grp), device_id_type=MESH,
+        recv_sem=reply_come, device_id=mate, device_id_type=MESH,
     )
     all_back.wait_recv()
     replies = back[...].reshape(ranks, 128)
@@ -358,6 +375,7 @@
     slots, width = centroid_init.shape
     prior = jnp.broadcast_to(prior_count[:, None], (slots, 128))
     vmem = pl.BlockSpec(memory_space=pltpu.VMEM)
+    hbm = pl.BlockSpec(memory_space=pltpu.HBM)
     smem = pl.BlockSpec(memory_space=pltpu.SMEM)
     bf16, f32, dma = jnp.bfloat16, jnp.float32, pltpu.SemaphoreType.DMA
     return pl.pallas_call(
@@ -366,14 +384,15 @@
             jax.ShapeDtypeStruct(assign.shape, f32),
             jax.ShapeDtypeStruct(centroid_init.shape, f32),
         ],
-        in_specs=[vmem] * 8 + [smem] + [vmem] * 3,
+        in_specs=[hbm] * 5 + [vmem] * 3 + [smem] + [vmem] * 3,
         out_specs=[vmem] * 2,
         scratch_shapes=[
             pltpu.VMEM((3 * channels, channels), bf16),
             pltpu.VMEM((2 * channels, channels), bf16),
             pltpu.VMEM((2 * channels, channels), bf16),
-            pltpu.VMEM((4,) + proj_weight.shape, bf16),
+            pltpu.VMEM((4,) + proj_weight.shape[::-1], bf16),
             pltpu.VMEM((16, channels), bf16),
+            pltpu.VMEM((steps, channels), bf16),
             pltpu.VMEM((channels // 128, steps + 8, 128), f32),
             pltpu.VMEM((channels // 128, steps // 2, 128), f32),
             pltpu.VMEM((channels // 128, steps // 4, 128), f32),
@@ -388,14 +407,14 @@
             pltpu.VMEM((256, 128), f32),
             pltpu.VMEM((ranks, 1, 128), f32),
             pltpu.VMEM((ranks, 1, 128), f32),
-            dma((4, 12)), dma((4, 6)), dma((4, 6)), dma, dma,
+            dma((4, 12)), dma((4, 6)), dma((4, 6)), dma((5,)), dma, dma,
             dma, dma, dma, dma((3,)), dma((3,)), dma, dma,
         ],
         compiler_params=pltpu.CompilerParams(
-            collective_id=0, has_side_effects=True, vmem_limit_bytes=48 * 1024 * 1024
+            collective_id=0, has_side_effects=True, vmem_limit_bytes=63 * 1024 * 1024
         ),
     )(
-        signal, conv5_weight, conv6_weight, conv7_weight, proj_weight, norm_gain[None], norm_bias[None],
+        signal, conv5_weight, conv6_weight, conv7_weight, proj_weight.T, norm_gain[None], norm_bias[None],
         proj_bias[None], rec_length, assign, centroid_init, prior,
     )
 

time: 111 us -> 103 us (0.928)
  Pallas kernels: 103 us -> 97.1 us
  local copies, waits for them, and re-layouts: 6.15 us -> 4.58 us
    pallas_call x1, Pallas kernels: 103 us -> 97.1 us  [shards(): pl.pallas_call(whole_kernel, out_shape=[jax.ShapeDtypeStruct(assign.shape...]
    unnamed x21 -> x8, local copies, waits for them, and re-layouts: 5.42 us -> 3.32 us
where the time goes in v4:
time: 103 us
  Pallas kernels  97.1 us (94%)
  local copies, waits for them, and re-layouts  4.58 us (4%)
  between operations  1.3 us (1%)
    pallas_call x1, Pallas kernels, shards(): pl.pallas_call(whole_kernel, out_shape=[jax.ShapeDtypeStruct(assign.shape...  97.1 us
    unnamed x8, local copies, waits for them, and re-layouts  3.32 us

profile of v4, /device:TPU:1, one launch (start us, length us, event | category | flops | bytes accessed | tf_op | source)
XLA Modules:
  0.0 103.0 jit_solution(11832140850739508086)
XLA Ops:
  1.3 0.0 copy-start
  1.3 0.7 copy-done
  2.0 0.0 copy-start.2
  2.0 0.6 broadcast_in_dim.17.bias_ref
  2.6 0.1 copy-done.2
  2.6 0.7 broadcast_in_dim.18.prior_ref
  3.3 97.1 %shard_map.131 = (f32[3,1,128]{2,1,0:T(1,128)}, f32[8,768]{1,0:T(8,128)}) custom-call(bf16[1024,512]{1,0:T(8,128)(2,1)} %bitcast.4, bf16[1536,128]{1,0:T(8,128)(2,1)} %a5.1, bf16[1024,128]{1,0:T(8,128)(2,1)} %a6.1, bf16[1024,128]{1,0:T(8,128)(2,1)} %a7.1, bf16[192,512]{1,0:T(8,128)(2,1)} %bitcast.5, f32[1,512]{1,0:T(1,128)} %bitcast.6, f32[1,512]{1,0:T(1,128)} %bitcast.7, ...), custom_call_target="tpu_custom_call" | custom-call | tf_op jit(solution)/shard_map/pallas_call | solution.py:381
  100.4 0.0 copy-start.1
  100.4 0.7 copy-done.1
  101.0 0.6 copy.17
  101.6 1.3 %copy.18 = f32[8,768]{1,0:T(8,128)} copy(f32[8,768]{1,0:T(8,128)} %get-tuple-element.5) | data formatting | bytes 49152
Async XLA Ops:
  1.3 0.7 copy-start
  2.0 0.7 copy-start.2
  100.4 0.7 copy-start.1

commit v5 on v4

--- a/solution.py
+++ b/solution.py
@@ -233,7 +233,7 @@
     @for_peers
     def _(peer):
         pltpu.make_async_remote_copy(
-            src_ref=sent.at[peer], dst_ref=got.at[rec], send_sem=go_sem, recv_sem=come_sem,
+            src_ref=sent.at[peer], dst_ref=got.at[rec], send_sem=go_sem, recv_sem=come_sem.at[level],
             device_id=(peer, grp), device_id_type=MESH,
         ).start()
 
@@ -242,9 +242,14 @@
     own.wait()
     every = pltpu.make_async_remote_copy(
         src_ref=sent.at[pl.ds(0, ranks - 1)], dst_ref=got.at[pl.ds(0, ranks - 1)], send_sem=go_sem,
-        recv_sem=come_sem, device_id=mate, device_id_type=MESH,
+        recv_sem=come_sem.at[0], device_id=mate, device_id_type=MESH,
     )
-    every.wait_recv()
+
+    def arrived(c, count):
+        pltpu.make_async_remote_copy(
+            src_ref=sent.at[pl.ds(0, count)], dst_ref=got.at[pl.ds(0, count)], send_sem=go_sem,
+            recv_sem=come_sem.at[c], device_id=mate, device_id_type=MESH,
+        ).wait_recv()
 
     shape = (lot, PIECES, 128)
     piece = lax.broadcasted_iota(jnp.int32, shape, 1)
@@ -275,7 +280,13 @@
         return sums, hits
 
     zero = jnp.zeros((256, 128), jnp.float32)
-    sums, hits = lax.fori_loop(0, 8, add_up, (zero, zero))
+    def next_level(i, carry):
+        c = lax.rem(level + i, 8)
+        arrived(c, lot)
+        return add_up(c, carry)
+
+    arrived(level, lot - 1)
+    sums, hits = lax.fori_loop(1, 8, next_level, add_up(level, (zero, zero)))
     part[0:144, :] = sums[0:144]
     for t in range(ITERS):
         part[144 + 8 * t : 152 + 8 * t, :] = hits[48 * t : 48 * t + 8]
@@ -408,7 +419,7 @@
             pltpu.VMEM((ranks, 1, 128), f32),
             pltpu.VMEM((ranks, 1, 128), f32),
             dma((4, 12)), dma((4, 6)), dma((4, 6)), dma((5,)), dma, dma,
-            dma, dma, dma, dma((3,)), dma((3,)), dma, dma,
+            dma, dma((8,)), dma, dma((3,)), dma((3,)), dma, dma,
         ],
         compiler_params=pltpu.CompilerParams(
             collective_id=0, has_side_effects=True, vmem_limit_bytes=63 * 1024 * 1024

time: 103 us -> 102 us (level)
  Pallas kernels: 97.1 us -> 95.7 us
    pallas_call x1, Pallas kernels: 97.1 us -> 95.7 us  [shards(): pl.pallas_call(whole_kernel, out_shape=[jax.ShapeDtypeStruct(assign.shape...]
where the time goes in v5:
time: 102 us
  Pallas kernels  95.7 us (94%)
  local copies, waits for them, and re-layouts  4.58 us (4%)
  between operations  1.3 us (1%)
    pallas_call x1, Pallas kernels, shards(): pl.pallas_call(whole_kernel, out_shape=[jax.ShapeDtypeStruct(assign.shape...  95.7 us
    unnamed x8, local copies, waits for them, and re-layouts  3.32 us

profile of v5, /device:TPU:1, one launch (start us, length us, event | category | flops | bytes accessed | tf_op | source)
XLA Modules:
  0.0 101.6 jit_solution(9605194933838509470)
XLA Ops:
  1.3 0.0 copy-start
  1.3 0.7 copy-done
  2.0 0.0 copy-start.2
  2.0 0.6 broadcast_in_dim.17.bias_ref
  2.6 0.1 copy-done.2
  2.6 0.7 broadcast_in_dim.18.prior_ref
  3.3 95.7 %shard_map.131 = (f32[3,1,128]{2,1,0:T(1,128)}, f32[8,768]{1,0:T(8,128)}) custom-call(bf16[1024,512]{1,0:T(8,128)(2,1)} %bitcast.4, bf16[1536,128]{1,0:T(8,128)(2,1)} %a5.1, bf16[1024,128]{1,0:T(8,128)(2,1)} %a6.1, bf16[1024,128]{1,0:T(8,128)(2,1)} %a7.1, bf16[192,512]{1,0:T(8,128)(2,1)} %bitcast.5, f32[1,512]{1,0:T(1,128)} %bitcast.6, f32[1,512]{1,0:T(1,128)} %bitcast.7, ...), custom_call_target="tpu_custom_call" | custom-call | tf_op jit(solution)/shard_map/pallas_call | solution.py:392
  99.0 0.0 copy-start.1
  99.0 0.7 copy-done.1
  99.7 0.6 copy.17
  100.2 1.3 %copy.18 = f32[8,768]{1,0:T(8,128)} copy(f32[8,768]{1,0:T(8,128)} %get-tuple-element.5) | data formatting | bytes 49152
Async XLA Ops:
  1.3 0.7 copy-start
  2.0 0.7 copy-start.2
  99.0 0.7 copy-start.1
